TPU v7x, 32 devices: a whole 2x2x4 slice. The times are simulated.
32 devices in a mesh: dp: 8 (over z, x), seq: 4 (over y, core).
Axes of the slice: x: 2, y: 2, z: 4, core: 2. Of those that a mesh axis runs over, the one named last changes fastest.
Arguments:
- tokens: bfloat16 [16384, 1024], P(('dp', 'seq')), may hold values from -6 to 6
- time_embed: bfloat16 [32, 1024], P(('dp', 'seq')), may hold values from -6 to 6
- lengths: int32 [32], P('dp'), may hold values from 0 to 475, as said below
- cotangent: bfloat16 [16384, 1024], P(('dp', 'seq')), may hold values from -6 to 6
- w_query: bfloat16 [1024, 1024], P('seq'), may hold values from -0.1875 to 0.1875
- w_key: bfloat16 [1024, 1024], P('seq'), may hold values from -0.1875 to 0.1875
- w_value: bfloat16 [1024, 1024], P('seq'), may hold values from -0.1875 to 0.1875
- w_out: bfloat16 [1024, 1024], P('seq'), may hold values from -0.75 to 0.75
- w_time: bfloat16 [1024, 1024], P('seq'), may hold values from -0.1875 to 0.1875
- w_in: bfloat16 [4096, 1024], P('seq'), may hold values from -0.1875 to 0.1875
- w_down: bfloat16 [4096, 1024], P('seq'), may hold values from -0.09375 to 0.09375
- b_query: bfloat16 [1024], replicated, may hold values from -3 to 3
- b_value: bfloat16 [1024], replicated, may hold values from -3 to 3
- b_out: bfloat16 [1024], replicated, may hold values from -3 to 3
- b_time: bfloat16 [1024], replicated, may hold values from -3 to 3
- b_in: bfloat16 [4096], replicated, may hold values from -3 to 3
- b_down: bfloat16 [1024], replicated, may hold values from -2 to 2
- gain_one: bfloat16 [1024], replicated, may hold values from 0.25 to 1.75
- shift_one: bfloat16 [1024], replicated, may hold values from -2 to 2
- gain_two: bfloat16 [1024], replicated, may hold values from 0.25 to 1.75
- shift_two: bfloat16 [1024], replicated, may hold values from -2 to 2
Outputs:
- layer_out: bfloat16 [16384, 1024], P(('dp', 'seq'))
- grad_tokens: bfloat16 [16384, 1024], P(('dp', 'seq'))
- grad_w_query: float32 [1024, 1024], P('seq')
- grad_w_key: float32 [1024, 1024], P('seq')
- grad_w_value: float32 [1024, 1024], P('seq')
- grad_w_out: float32 [1024, 1024], P('seq')
- grad_w_time: float32 [1024, 1024], P('seq')
- grad_w_in: float32 [4096, 1024], P('seq')
- grad_w_down: float32 [4096, 1024], P('seq')
- grad_b_query: float32 [1024], replicated
- grad_b_value: float32 [1024], replicated
- grad_b_out: float32 [1024], replicated
- grad_b_time: float32 [1024], replicated
- grad_b_in: float32 [4096], replicated
- grad_b_down: float32 [1024], replicated
- grad_gain_one: float32 [1024], replicated
- grad_shift_one: float32 [1024], replicated
- grad_gain_two: float32 [1024], replicated
- grad_shift_two: float32 [1024], replicated
Inputs may be any that keep to these rules, and one draw needn't show every extreme that they name: Item i's valid slots are its first lengths[i] + 25; every draw has an item of length 475 and one of length 0.
All inputs are finite; a program needn't handle non-finite values.
Results may differ from a plain program's by a relative error of at most 0.02.
Values may be sent and summed in bfloat16 or wider, within the bound.
A program may use at most 256 MiB of HBM per device.

v0:
```python
import functools

import jax
import jax.numpy as jnp
from jax import lax
from jax.experimental import pallas as pl
from jax.experimental.pallas import tpu as pltpu
from jax.sharding import PartitionSpec as P

HEAD_DIM = 64
BLOCK = 25
MESH = pl.DeviceIdType.MESH


norm_eps = 1e-05
neg_large = -1e30


def layer_norm(values, gain, shift):
    center = values - jnp.mean(values, axis=-1, keepdims=True)
    spread = lax.rsqrt(jnp.mean(center * center, axis=-1, keepdims=True) + norm_eps)
    return center * spread * gain + shift


def gelu_parts(values):
    half = 0.5 + 0.5 * lax.erf(values * 0.5**0.5)
    density = jnp.exp(-0.5 * values * values) * (0.5 / jnp.pi) ** 0.5
    return values * half, half + values * density


def _forward_kernel(sizes, *refs):
    n = len(sizes)
    given, (tokens, embed, rows_in, bias_in, keep) = refs[:n], refs[n : n + 5]
    outs = refs[n + 5 : 2 * n + 5]
    (resid_out, query_out, key_out, value_out, mixed_out, pre_out, hidden_out, slope_out, ffn_out, log_total) = refs[
        2 * n + 5 : 2 * n + 15
    ]
    full = refs[2 * n + 15 : 3 * n + 15]
    act, pre, first_low, hidden, slope, total = refs[3 * n + 15 : 3 * n + 21]
    load_sem, save_sem, act_sem, c_send, c_recv, y_send, y_recv, x_send, x_recv, f_send, f_recv, g_send, g_recv = refs[
        3 * n + 21 :
    ]
    f32, bf16 = jnp.float32, jnp.bfloat16
    w_time, w_query, w_key, w_value, w_out, w_in, w_down = full
    slots, width = tokens.shape
    pair = 2 * HEAD_DIM
    scale = HEAD_DIM**-0.5
    dp, me = lax.axis_index("dp"), lax.axis_index("seq")
    half = lax.rem(dp, 2)

    def home(a, shard):
        return full[a].at[pl.ds(pl.multiple_of(shard * sizes[a], sizes[a]), sizes[a]), :]

    loads = [pltpu.make_async_copy(given[a], home(a, me), load_sem.at[a]) for a in range(n)]
    for load in loads:
        load.start()
    core, across, side = (dp, me ^ 1), (dp, me ^ 2), (dp ^ 1, me)
    barrier = pltpu.get_barrier_semaphore()
    for peer in (core, across, side):
        pl.semaphore_signal(barrier, inc=1, device_id=peer, device_id_type=MESH)
    pl.semaphore_wait(barrier, 3)

    def remote(src, send, recv, peer):
        return pltpu.make_async_remote_copy(
            src_ref=src, dst_ref=src, send_sem=send, recv_sem=recv, device_id=peer, device_id_type=MESH
        )

    chunks, of = [], [[] for _ in sizes]
    for a, rows in enumerate(sizes):
        step = min(rows // 2, 128)
        for off in range(0, rows // 2, step):
            of[a].append(len(chunks))
            chunks.append((a, rows, off, step))

    def region(j, shard, part):
        a, rows, off, step = chunks[j]
        start = pl.multiple_of(shard * rows + part * (rows // 2) + off, 16)
        return full[a].at[pl.ds(start, step), :]

    saves = []

    def crossing(j):
        return remote(region(j, me, half), y_send.at[j], y_recv.at[j], across)

    def core_copy(a):
        return remote(home(a, me), c_send.at[a], c_recv.at[a], core)

    def sideways(j):
        return remote(region(j, me ^ 2, half), x_send.at[j], x_recv.at[j], side)

    def first_half(j):
        return remote(region(j, me ^ 2, half), f_send.at[j], f_recv.at[j], core)

    def second_half(j):
        return remote(region(j, me ^ 2, 1 - half), g_send.at[j], g_recv.at[j], core)

    for j, (a, rows, off, _) in enumerate(chunks):
        if off == 0:
            loads[a].wait()
            core_copy(a).start()
        crossing(j).start()

    def step(j):
        crossing(j).wait_recv()
        sideways(j).start()
        first_half(j).start()

    def turn(j):
        sideways(j).wait_recv()
        second_half(j).start()

    def arrived(j):
        first_half(j).wait_recv()
        second_half(j).wait_recv()

    def save(src, dst, sem):
        copy = pltpu.make_async_copy(src, dst, sem)
        copy.start()
        saves.append(copy)

    def complete(a):
        for j in of[a]:
            arrived(j)
        core_copy(a).wait_recv()
        save(full[a], outs[a], save_sem.at[a])

    def dot(a, b, dims):
        return lax.dot_general(a, b, (dims, ((), ())), preferred_element_type=f32)

    def bias(i):
        return rows_in[i : i + 1, :]

    tile = 256

    def tiles(extent, size, body):
        def run(i, carry):
            body(pl.ds(pl.multiple_of(i * size, size), size))
            return carry

        lax.fori_loop(0, extent // size, run, 0)

    def project(weight, i, row):
        def body(cols):
            value = dot(act[0], weight[:, cols], ((1,), (0,)))
            if row is not None:
                value += rows_in[row : row + 1, cols]
            act[i, :, cols] = value.astype(bf16)

        tiles(width, tile, body)
        save(act.at[i], (resid_out, query_out, key_out, value_out)[i], act_sem.at[i])

    step(0)
    step(1)
    turn(0)
    complete(0)
    time_proj = dot(embed[...], w_time[...], ((1,), (0,)))[0:1] + bias(0)

    def enter(r):
        value = tokens[r, :].astype(f32) + time_proj
        pre[r, :] = value
        act[0, r, :] = value.astype(bf16)

    tiles(slots, 64, enter)
    save(act.at[0], resid_out, act_sem.at[0])
    for j, (weight, row) in enumerate(((w_query, 1), (w_key, None), (w_value, 2))):
        step(j + 2)
        turn(j + 1)
        complete(j + 1)
        project(weight, j + 1, row)

    first = lax.broadcasted_iota(jnp.int32, (1, pair), 1) < HEAD_DIM

    def head_pair(p):
        cols = pl.ds(pl.multiple_of(p * pair, pair), pair)
        q2, k2, v2 = (act[i, :, cols] for i in (1, 2, 3))
        kept = keep[...] > 0
        found = []
        for h in range(2):
            mask = jnp.where(first == (h == 0), scale, 0.0)
            scores = jnp.where(kept, dot(k2, q2 * mask.astype(bf16), ((1,), (1,))), neg_large)
            top = jnp.max(scores, axis=0, keepdims=True)
            weights = jnp.exp(scores - top)
            norm = jnp.sum(weights, axis=0, keepdims=True)
            soft = (weights * (1.0 / norm)).astype(bf16)
            log_total[pl.ds(2 * p + h, 1), :] = top + jnp.log(norm)
            found.append(dot(v2, soft, ((0,), (0,))))
        mixed = jnp.concatenate([found[0][:HEAD_DIM], found[1][HEAD_DIM:]], axis=0)
        act[4, :, cols] = mixed.T.astype(bf16)

    beside = {0: (None, 4), 1: (5, None), 3: (6, 5), 5: (7, 6), 7: (8, 7)}

    def attend(p, carry):
        for at, (enters, turns) in beside.items():

            @pl.when(p == at)
            def _():
                if enters is not None:
                    step(enters)
                if turns is not None:
                    turn(turns)

        head_pair(p)
        return carry

    lax.fori_loop(0, width // pair, attend, 0)
    save(act.at[4], mixed_out, act_sem.at[4])
    complete(4)

    def attn_out(cols):
        pre[:, cols] += dot(act[4], w_out[:, cols], ((1,), (0,))) + rows_in[3:4, cols]

    tiles(width, tile, attn_out)
    step(9)
    turn(8)
    save(pre, pre_out, act_sem.at[5])

    def norm_rows(r):
        first_low[r, :] = layer_norm(pre[r, :], bias(4), bias(5)).astype(bf16)

    tiles(slots, 32, norm_rows)

    def feed_up(start, size):
        rows = pl.ds(pl.multiple_of(start, size), size)
        value = dot(first_low[...], w_in[rows, :], ((1,), (1,))) + bias_in[:, rows]
        up, lean = gelu_parts(value)
        hidden[:, rows] = up.astype(bf16)
        slope[:, rows] = lean.astype(bf16)

    share = sizes[5]

    def up_shard(shard):
        def run(i, carry):
            feed_up(shard * share + i * tile, tile)
            return carry

        lax.fori_loop(0, share // tile, run, 0)

    def down_shards(shards, opening):
        def body(cols):
            value = rows_in[6:7, cols] if opening else total[:, cols]
            for shard in shards:
                rows = pl.ds(pl.multiple_of(shard * share, share), share)
                value = value + dot(hidden[:, rows], w_down[rows, cols], ((1,), (0,)))
            total[:, cols] = value

        tiles(width, tile, body)

    def up_arrived(which):
        def run(i, carry):
            shard = (me ^ 2) ^ lax.rem(i, 2)
            feed_up(shard * share + lax.div(i, 2) * (share // 2) + which * tile, tile)
            return carry

        lax.fori_loop(0, 4, run, 0)

    up_shard(me)
    step(10)
    turn(9)
    core_copy(5).wait_recv()
    up_shard(me ^ 1)
    step(11)
    turn(10)
    core_copy(6).wait_recv()
    down_shards((me, me ^ 1), True)
    for j in (5, 6):
        arrived(j)
    up_arrived(0)
    step(12)
    turn(11)
    for j in (7, 8):
        arrived(j)
    save(w_in, outs[5], save_sem.at[5])
    up_arrived(1)
    turn(12)
    save(hidden, hidden_out, act_sem.at[6])
    save(slope, slope_out, act_sem.at[7])
    for j in of[6]:
        arrived(j)
    save(w_down, outs[6], save_sem.at[6])
    down_shards((me ^ 2, me ^ 3), False)
    save(total, ffn_out, act_sem.at[8])
    for copy in saves:
        copy.wait()
    for a in range(n):
        core_copy(a).wait_send()
    for j in range(len(chunks)):
        for copy in (crossing, sideways, first_half, second_half):
            copy(j).wait_send()


def gather_and_forward(arrays, tokens, embed, rows_in, bias_in, keep):
    sizes = tuple(a.shape[0] for a in arrays)
    n = len(arrays)
    m = sum(max(1, r // 256) for r in sizes)
    slots, width = tokens.shape
    units = 4 * sizes[5]
    bf16, f32 = jnp.bfloat16, jnp.float32
    dma, vmem = pltpu.SemaphoreType.DMA, pltpu.VMEM
    anywhere, inside = pl.BlockSpec(memory_space=pl.ANY), pl.BlockSpec(memory_space=pltpu.VMEM)
    wide = jax.ShapeDtypeStruct((slots, width), bf16)
    return pl.pallas_call(
        functools.partial(_forward_kernel, sizes),
        out_shape=[jax.ShapeDtypeStruct((4 * a.shape[0], a.shape[1]), a.dtype) for a in arrays]
        + [wide] * 5
        + [jax.ShapeDtypeStruct((slots, width), f32)]
        + [jax.ShapeDtypeStruct((slots, units), bf16)] * 2
        + [jax.ShapeDtypeStruct((slots, width), f32), jax.ShapeDtypeStruct((width // HEAD_DIM, slots), f32)],
        in_specs=[anywhere] * n + [inside] * 5,
        out_specs=[anywhere] * (n + 9) + [inside],
        scratch_shapes=[vmem((4 * a.shape[0], a.shape[1]), a.dtype) for a in arrays]
        + [
            vmem((5, slots, width), bf16),
            vmem((slots, width), f32),
            vmem((slots, width), bf16),
            vmem((slots, units), bf16),
            vmem((slots, units), bf16),
            vmem((slots, width), f32),
        ]
        + [dma((n,)), dma((n,)), dma((9,))]
        + [dma((n,))] * 2
        + [dma((m,))] * 8,
        compiler_params=pltpu.CompilerParams(
            collective_id=0, has_side_effects=True, vmem_limit_bytes=66_000_000
        ),
        name="gather_and_forward",
    )(*arrays, tokens, embed, rows_in, bias_in, keep)


def _row_loop(rows, step, body):
    def run(i, carry):
        body(pl.ds(pl.multiple_of(i * step, step), step))
        return carry

    lax.fori_loop(0, rows // step, run, 0)


def _backward_kernel(dp_n, slab, lag, heights, own_heights, *refs):
    n_terms = len(heights)
    terms = refs[:n_terms]
    (query, key, value, grad_mixed, w_query, w_key, w_value, log_total, keep, resid_t, grad_first, vec, embed) = refs[
        n_terms : n_terms + 13
    ]
    out, vec_out, rec_out, grad_tokens = refs[n_terms + 13 : n_terms + 17]
    (own, core_in, y_in, x_in, z_in, act, grads, weights, time_sum, v_own, v_core, v_y, v_x, v_z, v_sum) = refs[
        n_terms + 17 : n_terms + 32
    ]
    (load_sem, act_sem, w_sem, c_s, c_r, y_s, y_r, x_s, x_r, z_s, z_r, zg_s, zg_r, xg_s, xg_r, out_sem) = refs[
        n_terms + 32 : n_terms + 48
    ]
    vs, vr, ws, wr = refs[n_terms + 48 :]
    f32, bf16 = jnp.float32, jnp.bfloat16
    count = out.shape[0] // slab
    nz = dp_n // 2
    scale = HEAD_DIM**-0.5
    slots, width = query.shape
    pair = 2 * HEAD_DIM
    pairs = width // pair
    dp, me = lax.axis_index("dp"), lax.axis_index("seq")
    x, z, y, c = lax.rem(dp, 2), lax.div(dp, 2), lax.div(me, 2), lax.rem(me, 2)
    core, across, side = (dp, me ^ 1), (dp, me ^ 2), (dp ^ 1, me)
    others = [(lax.rem(z + o, nz) * 2 + x, me) for o in range(1, nz)]

    act_loads = [
        pltpu.make_async_copy(src, act.at[i], act_sem.at[i]) for i, src in enumerate((query, key, value, grad_mixed))
    ]
    w_loads = [pltpu.make_async_copy(src, weights.at[i], w_sem.at[i]) for i, src in enumerate((w_query, w_key, w_value))]
    for load in act_loads:
        load.start()
    barrier = pltpu.get_barrier_semaphore()
    for peer in [core, across, side] + others:
        pl.semaphore_signal(barrier, inc=1, device_id=peer, device_id_type=MESH)
    pl.semaphore_wait(barrier, 3 + len(others))

    def remote(src, dst, send, recv, peer):
        return pltpu.make_async_remote_copy(
            src_ref=src, dst_ref=dst, send_sem=send, recv_sem=recv, device_id=peer, device_id_type=MESH
        )

    hs = slab // 2
    ps = hs // nz
    rs = min(ps, 32)
    given = sum(heights)
    full = given // slab

    row = 0
    ahead = 5
    issues = []
    for term, height in zip(terms, heights):
        step = min(height, slab)
        for off in range(0, height, step):
            issues.append((term, off, (row + off) // slab, (row + off) % slab, step))
        row += height

    def issue(term, off, k, at, step):
        rows, place = pl.ds(off, step), pl.ds(at, step)
        remote(term.at[:, 1 - c, rows, :], core_in.at[k, :, place, :], c_s.at[k], c_r.at[k], core).start()
        sem = load_sem.at[k] if not isinstance(k, int) or k < full else load_sem.at[count]
        pltpu.make_async_copy(term.at[:, c, rows, :], own.at[k, :, place, :], sem).start()

    upfront = slab > own_heights
    for k, entry in enumerate(issues):
        if upfront or k < ahead:
            issue(*entry)

    def issue_later(k):
        start = 0
        for term, height in zip(terms, heights):
            first, last = start // slab, (start + height) // slab

            @pl.when((k >= first) & (k < last))
            def _():
                off = pl.multiple_of((k - first) * slab, slab)
                issue(term, off, k, 0, slab)

            start += height

    for load in w_loads:
        load.start()

    def core_copy(k):
        return remote(core_in.at[k], core_in.at[k], c_s.at[k], c_r.at[k], core)

    def y_copy(k):
        return remote(own.at[k, 1 - y], y_in.at[k], y_s.at[k], y_r.at[k], across)

    def x_copy(k):
        give = pl.ds(pl.multiple_of((1 - x) * hs, 16), hs)
        return remote(own.at[k, y, give], x_in.at[k], x_s.at[k], x_r.at[k], side)

    def z_copy(k, o):
        piece = pl.ds(pl.multiple_of(x * hs + lax.rem(z + o, nz) * ps, 16), ps)
        return remote(own.at[k, y, piece], z_in.at[k, o], z_s.at[k, o], z_r.at[k, o], others[o - 1])

    def zg_copy(k, o):
        mine = own.at[k, 1 - y, pl.ds(pl.multiple_of(x * hs + z * ps, 16), ps)]
        return remote(mine, mine, zg_s.at[k, o], zg_r.at[k, o], others[o - 1])

    def xg_copy(k):
        mine = own.at[k, 1 - y, pl.ds(pl.multiple_of(x * hs, 16), hs)]
        return remote(mine, mine, xg_s.at[k], xg_r.at[k], side)

    def out_copy(k):
        rows = pl.ds(pl.multiple_of(k * slab, slab), slab)
        return pltpu.make_async_copy(own.at[k, 1 - y], out.at[rows, :], out_sem.at[k])

    def stage_core(k):
        @pl.when(k < full)
        def _():
            pltpu.make_async_copy(own.at[k], own.at[k], load_sem.at[k]).wait()

        core_copy(k).wait_recv()

        def add(r):
            for p in range(2):
                own[k, p, r] = (own[k, p, r].astype(f32) + core_in[k, p, r].astype(f32)).astype(bf16)

        _row_loop(slab, 16, add)
        y_copy(k).start()

    def stage_y(k):
        y_copy(k).wait()

        def add(r):
            own[k, y, r] = (own[k, y, r].astype(f32) + y_in[k, r].astype(f32)).astype(bf16)

        _row_loop(slab, 32, add)
        x_copy(k).start()

    def stage_x(k):
        x_copy(k).wait_recv()

        def add(r):
            at = pl.ds(pl.multiple_of(x * hs + r.start, 16), r.size)
            own[k, y, at] = (own[k, y, at].astype(f32) + x_in[k, r].astype(f32)).astype(bf16)

        _row_loop(hs, rs, add)
        for o in range(1, nz):
            z_copy(k, o).start()

    def stage_z(k):
        for o in range(1, nz):
            z_copy(k, o).wait_recv()

        def add(r):
            at = pl.ds(pl.multiple_of(x * hs + z * ps + r.start, 16), r.size)
            total = own[k, y, at].astype(f32)
            for o in range(1, nz):
                total += z_in[k, o, r].astype(f32)
            own[k, 1 - y, at] = total.astype(bf16)

        _row_loop(ps, rs, add)
        for o in range(1, nz):
            zg_copy(k, o).start()

    def stage_zg(k):
        for o in range(1, nz):
            zg_copy(k, o).wait_recv()
        xg_copy(k).start()

    def stage_xg(k):
        xg_copy(k).wait_recv()
        out_copy(k).start()

    def dot(a, b, dims):
        return lax.dot_general(a, b, (dims, ((), ())), preferred_element_type=f32)

    def head_pair(p):
        cols = pl.ds(pl.multiple_of(p * pair, pair), pair)
        q2, k2, v2, g2 = (act[i, :, cols] for i in range(4))
        first = lax.broadcasted_iota(jnp.int32, (1, pair), 1) < HEAD_DIM
        kept = keep[...] > 0
        found = []
        for h in range(2):
            mask = jnp.where(first == (h == 0), 1.0, 0.0)
            q_h = q2 * (mask * scale).astype(bf16)
            g_h = g2 * mask.astype(bf16)
            scores = dot(k2, q_h, ((1,), (1,)))
            soft = jnp.where(kept, jnp.exp(scores - log_total[pl.ds(2 * p + h, 1), :]), 0.0)
            grad_soft = dot(v2, g_h, ((1,), (1,)))
            inner = jnp.sum(soft * grad_soft, axis=0, keepdims=True)
            grad_scores = (soft * (grad_soft - inner)).astype(bf16)
            found.append(
                (
                    dot(k2, grad_scores, ((0,), (0,))),
                    dot(grad_scores, q2, ((1,), (0,))),
                    dot(soft.astype(bf16), g2, ((1,), (0,))),
                )
            )
        q_t = jnp.concatenate([found[0][0][:HEAD_DIM], found[1][0][HEAD_DIM:]], axis=0)
        grad_q = (q_t.T * scale).astype(bf16)
        grad_k = (jnp.where(first, found[0][1], found[1][1]) * scale).astype(bf16)
        grad_v = jnp.where(first, found[0][2], found[1][2]).astype(bf16)
        grads[0, :, cols] = grad_q
        grads[1, :, cols] = grad_k
        grads[2, :, cols] = grad_v
        v_own[0:1, cols] = jnp.sum(grad_q.astype(f32), axis=0, keepdims=True)
        v_own[1:2, cols] = jnp.sum(grad_v.astype(f32), axis=0, keepdims=True)

    def term(m):
        step = min(own_heights, slab)
        for cc, mine in ((1 - c, False), (c, True)):
            for p in range(2):
                left = resid_t[pl.ds(pl.multiple_of((p * 2 + cc) * own_heights, own_heights), own_heights), :]
                tile = dot(left, grads[m], ((1,), (0,))).astype(bf16)
                if not mine:
                    act[m, p * own_heights : (p + 1) * own_heights] = tile
                for off in range(0, own_heights, step):
                    start = given + m * own_heights + off
                    k, at = lax.div(start, slab), pl.multiple_of(lax.rem(start, slab), step)
                    if mine:
                        own[k, p, pl.ds(at, step)] = tile[off : off + step]
                    else:
                        src = act.at[m, pl.ds(p * own_heights + off, step), :]
                        dst = core_in.at[k, p, pl.ds(at, step), :]
                        remote(src, dst, c_s.at[k], c_r.at[k], core).start()

    blocks = 4
    block = slots // blocks

    def resid_rows(r):
        rows = pl.ds(pl.multiple_of(r * block, block), block)
        total = grad_first[rows, :]
        for m in range(3):
            total += dot(grads[m, rows, :], weights[m], ((1,), (1,)))
        grad_tokens[rows, :] = total.astype(bf16)
        time_sum[...] += jnp.sum(total, axis=0, keepdims=True)

    v_half = v_core.shape[0]
    v_mine = pl.ds(pl.multiple_of(c * v_half, v_half), v_half)
    v_given = pl.ds(pl.multiple_of((1 - c) * v_half, v_half), v_half)

    def v_copy(i):
        peers = [core, across, side] + others + [core]
        if i == 0:
            src, dst = v_own.at[v_given], v_core
        elif i == 2 + nz:
            src = dst = vec_out.at[v_mine]
        else:
            src, dst = v_sum.at[min(i, 3) - 1], v_z.at[i - 2] if i > 2 else (v_y, v_x)[i - 1]
        return remote(src, dst, vs.at[i], vr.at[i], peers[i])

    def v_stage(i):
        if i == 0:
            v_copy(0).start()
        elif i <= 3:
            v_copy(i - 1).wait_recv()
            before = v_own[v_mine] if i == 1 else v_sum[i - 2]
            v_sum[i - 1] = before + (v_core, v_y, v_x)[i - 1][...]
            for j in range(i, i + 1 if i < 3 else 2 + nz):
                v_copy(j).start()
        elif i == 4:
            total = v_sum[2]
            for o in range(1, nz):
                v_copy(2 + o).wait_recv()
                total = total + v_z[o]
            vec_out[v_mine] = total
            v_copy(2 + nz).start()
        else:
            v_copy(2 + nz).wait_recv()

    def w_copy(q, i):
        peers = [across, side] + others + [core]
        if i == 0:
            part = rec_out.at[q, dp, y, c]
        elif i == 1:
            part = rec_out.at[q, dp, :, c]
        elif i < 1 + nz:
            part = rec_out.at[q, pl.ds(z * 2, 2), :, c]
        else:
            part = rec_out.at[q, :, :, c]
        return remote(part, part, ws.at[q, i], wr.at[q, i], peers[i])

    def w_stage(q, i):
        if i == 0:
            if q == 0:
                rec_out[0, dp, y, c] = embed[...]
            else:
                rounded = time_sum[...].astype(bf16).astype(f32)
                lanes = embed.shape[-1]
                for j in range(width // lanes):
                    rec_out[1, dp, y, c, j : j + 1, :] = rounded[:, j * lanes : (j + 1) * lanes]
            w_copy(q, 0).start()
        elif i < 3:
            w_copy(q, i - 1).wait_recv()
            for j in range(i, i + 1 if i == 1 else 1 + nz):
                w_copy(q, j).start()
        elif i == 3:
            for o in range(1, nz):
                w_copy(q, 1 + o).wait_recv()
            w_copy(q, 1 + nz).start()
        else:
            w_copy(q, 1 + nz).wait_recv()

    stages = [stage_y, stage_x, stage_z, stage_zg, stage_xg]
    n_units = pairs + 3 + blocks
    base = 0 if slab <= own_heights else pairs + 4
    small = [(pairs + at, functools.partial(v_stage, i)) for i, at in enumerate((0, 2, 5, 7, 9, 10))]
    for q, first in ((0, 0), (1, n_units)):
        small += [(first + at, functools.partial(w_stage, q, i)) for i, at in enumerate((0, 3, 5, 7, 8))]
    ticks = max([base + count + lag * (len(stages) - 1)] + [at + 1 for at, _ in small])
    v_own[...] = vec[...]
    time_sum[...] = jnp.zeros_like(time_sum)
    for load in act_loads:
        load.wait()

    def tick(t, carry):
        @pl.when(t < pairs)
        def _():
            head_pair(t)

        @pl.when((t >= pairs) & (t < pairs + 3))
        def _():
            term(t - pairs)

        @pl.when(t == pairs + 3)
        def _():
            for load in w_loads:
                load.wait()

        @pl.when((t >= pairs + 3) & (t < n_units))
        def _():
            resid_rows(t - pairs - 3)

        if row > full * slab:

            @pl.when(t == base)
            def _():
                part = own.at[full, :, pl.ds(0, row - full * slab), :]
                pltpu.make_async_copy(part, part, load_sem.at[count]).wait()

        if not upfront:
            issue_later(t - base + ahead)

        for i in range(3):
            k = t - base + i

            @pl.when((k < count) & ((t == base) | ((t > base) & (i == 2))))
            def _():
                stage_core(k)

        for d, stage in enumerate(stages):
            k = t - base - d * lag

            @pl.when((k >= 0) & (k < count))
            def _():
                stage(k)

        for at, run in small:
            pl.when(t == at)(run)

        return carry

    lax.fori_loop(0, ticks, tick, 0)

    def finish(k, carry):
        core_copy(k).wait_send()
        x_copy(k).wait_send()
        for o in range(1, nz):
            z_copy(k, o).wait_send()
            zg_copy(k, o).wait_send()
        xg_copy(k).wait_send()
        out_copy(k).wait()
        return carry

    lax.fori_loop(0, count, finish, 0)
    for i in range(3 + nz):
        v_copy(i).wait_send()
    for i in range(2 + nz):
        for q in range(2):
            w_copy(q, i).wait_send()


def attend_and_reduce(dp_n, terms, acts, weights, log_total, keep, resid_t, grad_first, vec, embed):
    slots, width = acts[0].shape
    heights = tuple(t.shape[2] for t in terms)
    own_heights = width // 4
    rows = sum(heights) + 3 * own_heights
    slab = max(128, 16 * dp_n)
    count, nz = rows // slab, dp_n // 2
    bf16, f32 = jnp.bfloat16, jnp.float32
    dma, vmem = pltpu.SemaphoreType.DMA, pltpu.VMEM
    v_shape = vec.shape
    anywhere, inside = pl.BlockSpec(memory_space=pl.ANY), pl.BlockSpec(memory_space=pltpu.VMEM)
    half_shape = (v_shape[0] // 2, width)
    return pl.pallas_call(
        functools.partial(_backward_kernel, dp_n, slab, 1, heights, own_heights),
        out_shape=[
            jax.ShapeDtypeStruct((rows, width), bf16),
            jax.ShapeDtypeStruct(v_shape, f32),
            jax.ShapeDtypeStruct((2, dp_n, 2, 2) + embed.shape, f32),
            jax.ShapeDtypeStruct((slots, width), bf16),
        ],
        in_specs=[anywhere] * (len(terms) + 7) + [inside] * 6,
        out_specs=[anywhere, inside, inside, inside],
        scratch_shapes=[
            vmem((count, 2, slab, width), bf16),
            vmem((count, 2, slab, width), bf16),
            vmem((count, slab, width), bf16),
            vmem((count, slab // 2, width), bf16),
            vmem((count, nz, slab // 2 // nz, width), bf16),
            vmem((4, slots, width), bf16),
            vmem((3, slots, width), bf16),
            vmem((3, width, width), bf16),
            vmem((1, width), f32),
            vmem(v_shape, f32),
            vmem(half_shape, f32),
            vmem(half_shape, f32),
            vmem(half_shape, f32),
            vmem((nz,) + half_shape, f32),
            vmem((3,) + half_shape, f32),
        ]
        + [dma((count + 1,)), dma((4,)), dma((3,))]
        + [dma((count,))] * 6
        + [dma((count, nz))] * 4
        + [dma((count,))] * 3
        + [dma((3 + nz,))] * 2
        + [dma((2, 2 + nz))] * 2,
        compiler_params=pltpu.CompilerParams(collective_id=1, has_side_effects=True, vmem_limit_bytes=66_000_000),
        name="attend_and_reduce",
    )(*terms, *acts, *weights, log_total, keep, resid_t, grad_first, vec, embed)


def local(
    dp_n,
    tokens,
    time_embed,
    lengths,
    cotangent,
    w_query,
    w_key,
    w_value,
    w_out,
    w_time,
    w_in,
    w_down,
    b_query,
    b_value,
    b_out,
    b_time,
    b_in,
    b_down,
    gain_one,
    shift_one,
    gain_two,
    shift_two,
):
    f32, bf16 = jnp.float32, jnp.bfloat16
    seq_rank = lax.axis_index("seq")
    item_count = time_embed.shape[0]
    token_count = tokens.shape[0]
    slot_count = token_count // item_count
    width = tokens.shape[1]
    rows = w_time.shape[0]

    def mm(a, b, dims):
        return lax.dot_general(a, b, (dims, ((), ())), preferred_element_type=f32)

    own_lengths = lax.dynamic_slice_in_dim(lengths, seq_rank * item_count, item_count, 0)
    slot_index = lax.broadcasted_iota(jnp.int32, (item_count, slot_count), 1)
    own_valid = slot_index < own_lengths[:, None] + BLOCK
    row_keep = own_valid.reshape(token_count, 1).astype(f32)
    rows_in = jnp.stack([b_time, b_query, b_value, b_out, gain_one, shift_one, b_down, b_down]).astype(f32)
    (
        _,
        full_query,
        full_key,
        full_value,
        full_out,
        full_in,
        full_down,
        resid_low,
        query_rows,
        key_rows,
        value_rows,
        mixed_rows,
        first_in,
        hidden_low,
        gelu_slope,
        ffn_out,
        log_total,
    ) = gather_and_forward(
        [w_time, w_query, w_key, w_value, w_out, w_in, w_down],
        tokens,
        jnp.broadcast_to(time_embed, (16, width)),
        rows_in,
        b_in.astype(f32).reshape(1, -1),
        row_keep,
    )
    first_norm, first_pull = jax.vjp(
        layer_norm, first_in, gain_one.astype(f32), shift_one.astype(f32)
    )
    first_low = first_norm.astype(bf16)
    second_norm, second_pull = jax.vjp(
        layer_norm, first_norm + ffn_out, gain_two.astype(f32), shift_two.astype(f32)
    )
    layer_out = (second_norm * row_keep).astype(bf16)
    grad_second_in, grad_gain_two, grad_shift_two = second_pull(cotangent.astype(f32) * row_keep)
    grad_ffn = grad_second_in.astype(bf16)
    grad_hidden = mm(grad_ffn, full_down, ((1,), (1,)))
    grad_pre = (grad_hidden * gelu_slope).astype(bf16)
    grad_first = grad_second_in + mm(grad_pre, full_in, ((1,), (0,)))
    term_in = mm(grad_pre, first_low, ((0,), (0,))).astype(bf16)
    term_down = mm(hidden_low, grad_ffn, ((0,), (0,))).astype(bf16)
    grad_first_in, grad_gain_one, grad_shift_one = first_pull(grad_first)
    grad_attn = grad_first_in.astype(bf16)
    grad_mixed = mm(grad_attn, full_out, ((1,), (1,))).astype(bf16)
    terms = [
        term_down,
        term_in,
        mm(mixed_rows, grad_attn, ((0,), (0,))).astype(bf16),
    ]
    zero = jnp.zeros((width,), f32)
    vec = jnp.stack(
        [
            zero,
            zero,
            jnp.sum(grad_attn, axis=0, dtype=f32),
            jnp.sum(grad_ffn, axis=0, dtype=f32),
            grad_gain_one,
            grad_shift_one,
            grad_gain_two,
            grad_shift_two,
        ]
    )
    vec = jnp.concatenate([vec, jnp.sum(grad_pre, axis=0, dtype=f32).reshape(-1, width)], axis=0)
    vec = jnp.pad(vec, ((0, -vec.shape[0] % 8), (0, 0)))
    sums, vectors, every, grad_tokens = attend_and_reduce(
        dp_n,
        [t.reshape(2, 2, -1, width) for t in terms],
        [query_rows, key_rows, value_rows, grad_mixed],
        [full_query, full_key, full_value],
        log_total,
        row_keep,
        resid_low.T,
        grad_first_in,
        vec,
        time_embed.astype(f32).reshape(-1, 128),
    )
    time_rows, time_grads = every.reshape(2, -1, width).astype(bf16)
    own_columns = lax.dynamic_slice_in_dim(time_rows, seq_rank * rows, rows, 1)
    grad_w_time = mm(own_columns, time_grads, ((0,), (0,)))
    grad_b_time = jnp.sum(time_grads, axis=0, dtype=f32)
    grad_b_in = vectors[8 : 8 + b_in.shape[0] // width].reshape(-1)
    sums = sums.astype(f32)
    down_rows, in_rows = (t.shape[0] // 4 for t in terms[:2])
    ends = [0, down_rows, down_rows + in_rows]
    ends += [ends[-1] + rows * i for i in range(1, 5)]
    share_down, share_in, share_out, share_q, share_k, share_v = (
        sums[lo:hi] for lo, hi in zip(ends[:-1], ends[1:])
    )
    return (
        layer_out,
        grad_tokens,
        share_q,
        share_k,
        share_v,
        share_out,
        grad_w_time,
        share_in,
        share_down,
        vectors[0],
        vectors[1],
        vectors[2],
        grad_b_time,
        grad_b_in,
        vectors[3],
        vectors[4],
        vectors[5],
        vectors[6],
        vectors[7],
    )


def solution(mesh):
    in_specs = (
        P(("dp", "seq"), None),
        P(("dp", "seq"), None),
        P("dp"),
        P(("dp", "seq"), None),
        P("seq", None),
        P("seq", None),
        P("seq", None),
        P("seq", None),
        P("seq", None),
        P("seq", None),
        P("seq", None),
        P(),
        P(),
        P(),
        P(),
        P(),
        P(),
        P(),
        P(),
        P(),
        P(),
    )
    out_specs = (
        P(("dp", "seq"), None),
        P(("dp", "seq"), None),
        P("seq", None),
        P("seq", None),
        P("seq", None),
        P("seq", None),
        P("seq", None),
        P("seq", None),
        P("seq", None),
        P(),
        P(),
        P(),
        P(),
        P(),
        P(),
        P(),
        P(),
        P(),
        P(),
    )
    return jax.shard_map(functools.partial(local, mesh.shape["dp"]), mesh=mesh, in_specs=in_specs, out_specs=out_specs, check_vma=False)
```

profile of v0, /device:TPU:0, one launch (start us, length us, event | category | flops | bytes accessed | tf_op | source)
XLA Modules:
  0.0 357.7 jit_solution(12623656506447967182)
XLA Ops:
  0.7 1.2 dynamic_slice.8
  2.6 0.7 fusion.9.refs_11_
  3.3 1.4 fusion.29
  4.7 0.6 broadcast_in_dim.13.refs_8_
  5.3 0.7 stack.35
  6.0 0.7 stack.36
  6.6 0.7 stack.37
  7.3 0.7 stack.38
  8.0 0.7 stack.39
  8.7 0.7 stack.40
  9.4 0.7 stack.41
  10.1 0.1 stack.42
  10.1 0.6 convert_element_type.76.refs_9_
  10.8 1.3 reshape.176
  12.1 98.8 %gather_and_forward.1 = (bf16[1024,1024]{1,0:T(8,128)(2,1)}, bf16[1024,1024]{1,0:T(8,128)(2,1)}, bf16[1024,1024]{1,0:T(8,128)(2,1)}, bf16[1024,1024]{1,0:T(8,128...) custom-call(bf16[256,1024]{1,0:T(8,128)(2,1)} %refs_0_.1, ...), custom_call_target="tpu_custom_call" | custom-call | tf_op jit(solution)/shard_map/gather_and_forward/pallas_call | solution.py:301
  110.9 0.0 copy-start
  110.9 0.0 copy-start.8
  110.9 0.0 copy-start.9
  110.9 1.9 reduce_sum.140
  112.8 0.0 copy-start.3
  112.9 0.3 copy-done
  113.1 0.3 multiply_reduce_fusion.5
  113.5 0.0 copy-done.8
  113.5 0.0 copy-done.9
  113.5 1.0 copy-done.3
  114.5 0.7 fusion.23
  115.2 0.0 copy-start.2
  115.2 0.3 multiply_reduce_fusion.4
  115.6 0.3 copy-done.10
  115.9 0.6 copy-done.2
  116.4 0.9 multiply_reduce_fusion
  117.4 0.0 copy-done.11
  117.4 0.0 copy-start.13
  117.4 2.0 fusion.22
  119.4 0.2 convert_reduce_fusion.1
  119.7 0.3 copy-done.13
  120.0 9.5 %convert_reduce_fusion = (f32[4096]{0:T(1024)S(1)}, bf16[512,4096]{1,0:T(8,128)(2,1)}) fusion(bf16[512,4096]{1,0:T(8,128)(2,1)S(1)} %copy-done.13, bf16[512,1024]{1,0:T(8,128)(2,1)S(1)} %get-tuple-element.66, bf16[4096,1024]{1,0:T(8,128)(2,1)} %get-tuple-element.42), kind=kOutput, calls=%fused_computation | convolution fusion | flops 4305448960 | bytes 17842176 | tf_op jit(solution)/shard_map/dot_general | solution.py:796
  129.5 8.8 %multiply_reduce_fusion.1 = (f32[1024]{0:T(1024)S(1)}, f32[512]{0:T(512)S(1)}, f32[1024]{0:T(1024)S(1)}, f32[512,1024]{1,0:T(8,128)S(1)}) fusion(f32[512,1024]{1,0:T(8,128)S(1)} %copy-done, f32[512]{0:T(512)S(1)} %fusion.16, f32[512]{0:T(512)S(1)} %broadcast_multiply_fusion.1, f32[1024]{0:T(1024)S(1)} %convert_element_type.78, ...), kind=kOutput, calls=%fused_computation.7 | convolution fusion | flops 4300207616 | bytes 18894848 | tf_op jit(solution)/shard_map/dot_general | solution.py:796
  138.3 0.7 fusion.21
  139.0 1.6 convert_reduce_fusion.2
  140.6 0.1 concatenate.7
  140.7 0.6 pad.4.refs_14_
  141.3 4.6 %convolution_convert_fusion.3.refs_6_ = bf16[512,1024]{1,0:T(8,128)(2,1)} fusion(bf16[1024,1024]{1,0:T(8,128)(2,1)} %get-tuple-element.49, f32[512,1024]{1,0:T(8,128)} %get-tuple-element.68.refs_13_), kind=kOutput, calls=%fused_computation.24 | convolution fusion | flops 1074790400 | bytes 5242880 | tf_op jit(solution)/shard_map/dot_general | solution.py:796
  146.0 0.0 copy-done.1
  146.0 0.0 copy-done.14
  146.0 2.6 convolution_convert_fusion.2
  148.6 0.0 copy-done.15
  148.6 7.2 %convolution_convert_fusion = bf16[4096,1024]{1,0:T(8,128)(2,1)} fusion(bf16[512,4096]{1,0:T(8,128)(2,1)S(1)} %copy-done.15, f32[512,1024]{1,0:T(8,128)S(1)} %copy-done, f32[1024]{0:T(1024)S(1)} %convert_element_type.79, f32[1024]{0:T(1024)S(1)} %convert_element_type.78, f32[512]{0:T(512)S(1)} %fusion.16, f32[512]{0:T(512)S(1)} %broadcast_multiply_fusion.1), kind=kOutput, calls=%fused_computation.2 | convolution fusion | flops 4301783040 | bytes 14692352 | tf_op jit(solution)/shard_map/dot_general | solution.py:796
  155.8 0.0 copy-done.12
  155.8 6.8 %convolution_convert_fusion.1 = bf16[4096,1024]{1,0:T(8,128)(2,1)} fusion(bf16[512,4096]{1,0:T(8,128)(2,1)S(1)} %copy-done.12, bf16[512,1024]{1,0:T(8,128)(2,1)S(1)} %get-tuple-element.66), kind=kOutput, calls=%fused_computation.3 | convolution fusion | flops 4299161600 | bytes 13631488 | tf_op jit(solution)/shard_map/dot_general | solution.py:796
  162.6 0.0 copy-done.4
  162.6 1.3 copy.40
  163.9 179.0 %attend_and_reduce.1 = (bf16[3072,1024]{1,0:T(8,128)(2,1)}, f32[16,1024]{1,0:T(8,128)}, f32[2,8,2,2,8,128]{5,4,3,2,1,0:T(8,128)}, bf16[512,1024]{1,0:T(8,128)(2,1)}) custom-call(bf16[2,2,1024,1024]{3,2,1,0:T(8,128)(2,1)} %bitcast.47, bf16[2,2,1024,1024]{3,2,1,0:T(8,128)(2,1)} %bitcast.46, bf16[2,2,256,1024]{3,2,1,0:T(8,128)(2,1)} %bitcast.49, ...), custom_call_target="tpu_custom_call" | custom-call | tf_op jit(solution)/shard_map/attend_and_reduce/pallas_call | solution.py:725
  343.0 0.0 copy-start.6
  343.0 6.7 %fusion.25 = (f32[1024,1024]{1,0:T(8,128)}, f32[1024,1024]{1,0:T(8,128)}) fusion(bf16[3072,1024]{1,0:T(8,128)(2,1)} %get-tuple-element.56), kind=kLoop, calls=%fused_computation.58 | loop fusion | bytes 16777216 | tf_op jit(solution)/shard_map/slice | solution.py:889
  349.7 0.0 copy-done.6
  349.8 1.3 fusion.10
  351.1 3.8 %fusion.26 = (f32[256,1024]{1,0:T(8,128)}, f32[256,1024]{1,0:T(8,128)}, f32[256,1024]{1,0:T(8,128)}, f32[256,1024]{1,0:T(8,128)}) fusion(bf16[3072,1024]{1,0:T(8,128)(2,1)} %get-tuple-element.56), kind=kLoop, calls=%fused_computation.59 | loop fusion | bytes 8388608 | tf_op jit(solution)/shard_map/slice | solution.py:889
  354.9 0.6 convert_reduce_fusion.3
  355.5 0.0 copy-done.7
  355.5 0.6 fusion.28
  356.1 0.6 copy.49
  356.7 0.0 copy-done.5
  356.7 1.0 copy.51
  (28 shorter events, 0.2 us)
Async XLA Ops:
  110.9 2.2 copy-start
  110.9 2.6 copy-start.8
  110.9 2.6 copy-start.9
  112.8 1.7 copy-start.3
  115.2 0.7 copy-start.10
  115.2 1.2 copy-start.2
  115.6 1.8 copy-start.11
  117.4 2.6 copy-start.13
  141.3 4.6 %copy-start.1 = (f32[512,1024]{1,0:T(8,128)S(1)}, f32[512,1024]{1,0:T(8,128)}, u32[]{:S(2)}) copy-start(f32[512,1024]{1,0:T(8,128)} %get-tuple-element.68.refs_13_) | copy-start | bytes 6291460
  141.3 4.6 %copy-start.14 = (bf16[512,1024]{1,0:T(8,128)(2,1)S(1)}, bf16[512,1024]{1,0:T(8,128)(2,1)}, u32[]{:S(2)}) copy-start(bf16[512,1024]{1,0:T(8,128)(2,1)} %get-tuple-element.44) | copy-start | bytes 3145732
  146.0 2.6 copy-start.15
  148.6 7.2 %copy-start.12 = (bf16[512,4096]{1,0:T(8,128)(2,1)S(1)}, bf16[512,4096]{1,0:T(8,128)(2,1)}, u32[]{:S(2)}) copy-start(bf16[512,4096]{1,0:T(8,128)(2,1)} %get-tuple-element.41) | copy-start | bytes 12582916
  155.8 6.8 %copy-start.4 = (bf16[512,1024]{1,0:T(8,128)(2,1)S(1)}, bf16[512,1024]{1,0:T(8,128)(2,1)}, u32[]{:S(2)}) copy-start(bf16[512,1024]{1,0:T(8,128)(2,1)} %get-tuple-element.54) | copy-start | bytes 3145732
  343.0 6.7 %copy-start.6 = (f32[2,8,2,2,8,128]{5,4,3,2,1,0:T(8,128)S(1)}, f32[2,8,2,2,8,128]{5,4,3,2,1,0:T(8,128)}, u32[]{:S(2)}) copy-start(f32[2,8,2,2,8,128]{5,4,3,2,1,0:T(8,128)} %get-tuple-element.57) | copy-start | bytes 786436
  351.1 4.4 %copy-start.7 = (f32[16,1024]{1,0:T(8,128)S(1)}, f32[16,1024]{1,0:T(8,128)}, u32[]{:S(2)}) copy-start(f32[16,1024]{1,0:T(8,128)} %get-tuple-element.58) | copy-start | bytes 196612
  351.1 5.7 %copy-start.5 = (bf16[512,1024]{1,0:T(8,128)(2,1)S(1)}, bf16[512,1024]{1,0:T(8,128)(2,1)}, u32[]{:S(2)}) copy-start(bf16[512,1024]{1,0:T(8,128)(2,1)} %get-tuple-element.117) | copy-start | bytes 3145732
where the time goes:
time: 358 us
  Pallas kernels  278 us (78%)
  matrix products  40.9 us (11%)
  local copies, waits for them, and re-layouts  24 us (7%)
  other arithmetic  13.5 us (4%)
    pallas_call x1, Pallas kernels, attend_and_reduce(): pl.pallas_call(functools.partial(_backward_kernel, dp_n, slab, 1, heights...  179 us
    pallas_call x1, Pallas kernels, gather_and_forward(): pl.pallas_call(functools.partial(_forward_kernel, sizes), out_shape=[jax....  98.8 us
    dot_general x7, matrix products, mm(): return lax.dot_general(a, b, (dims, ((), ())), preferred_element_type=f32)  40.9 us
    slice x2, local copies, waits for them, and re-layouts, local(): sums[lo:hi]  10.5 us

commit v1 on v0

--- a/solution.py
+++ b/solution.py
@@ -334,20 +334,14 @@
     lax.fori_loop(0, rows // step, run, 0)
 
 
-def _backward_kernel(dp_n, slab, lag, heights, own_heights, *refs):
-    n_terms = len(heights)
-    terms = refs[:n_terms]
-    (query, key, value, grad_mixed, w_query, w_key, w_value, log_total, keep, resid_t, grad_first, vec, embed) = refs[
-        n_terms : n_terms + 13
-    ]
-    out, vec_out, rec_out, grad_tokens = refs[n_terms + 13 : n_terms + 17]
-    (own, core_in, y_in, x_in, z_in, act, grads, weights, time_sum, v_own, v_core, v_y, v_x, v_z, v_sum) = refs[
-        n_terms + 17 : n_terms + 32
-    ]
-    (load_sem, act_sem, w_sem, c_s, c_r, y_s, y_r, x_s, x_r, z_s, z_r, zg_s, zg_r, xg_s, xg_r, out_sem) = refs[
-        n_terms + 32 : n_terms + 48
-    ]
-    vs, vr, ws, wr = refs[n_terms + 48 :]
+def _backward_kernel(dp_n, slab, lag, *refs):
+    (hidden, slope, w_down, w_in, second, first_in, query, key, value, mixed, w_out, w_query, w_key, w_value) = refs[:14]
+    (grad_ffn_in, first_low_in, resid_in, log_total, keep, gain, vec, embed) = refs[14:22]
+    out, vec_out, rec_out, grad_tokens = refs[22:26]
+    (own, core_in, y_in, x_in, z_in, act, grads, weights, pieces, chunk_w, acc, before) = refs[26:38]
+    (time_sum, v_own, v_core, v_y, v_x, v_z, v_sum) = refs[38:45]
+    (piece_sem, act_sem, w_sem, f_sem, c_s, c_r, y_s, y_r, x_s, x_r, z_s, z_r, zg_s, zg_r, xg_s, xg_r, out_sem) = refs[45:62]
+    vs, vr, ws, wr = refs[62:]
     f32, bf16 = jnp.float32, jnp.bfloat16
     count = out.shape[0] // slab
     nz = dp_n // 2
@@ -355,16 +349,45 @@
     slots, width = query.shape
     pair = 2 * HEAD_DIM
     pairs = width // pair
+    share = w_in.shape[0] // 4
+    tile = width // 4
+    groups = share // tile
+    fine = slab <= tile
+    subs = tile // slab if fine else 1
+    part = min(slab, tile)
     dp, me = lax.axis_index("dp"), lax.axis_index("seq")
     x, z, y, c = lax.rem(dp, 2), lax.div(dp, 2), lax.div(me, 2), lax.rem(me, 2)
     core, across, side = (dp, me ^ 1), (dp, me ^ 2), (dp ^ 1, me)
     others = [(lax.rem(z + o, nz) * 2 + x, me) for o in range(1, nz)]
 
+    def shard_of(i):
+        return lax.rem(i, 2) * 2 + lax.rem(1 - c + lax.div(i, 2), 2)
+
+    def chunk_loads(u):
+        start = pl.multiple_of(shard_of(lax.rem(u, 4)) * share + lax.div(u, 4) * tile, tile)
+        rows, slot = pl.ds(start, tile), lax.rem(u, 2)
+        return [
+            pltpu.make_async_copy(hidden.at[:, rows], pieces.at[slot, 0], piece_sem.at[slot, 0]),
+            pltpu.make_async_copy(slope.at[:, rows], pieces.at[slot, 1], piece_sem.at[slot, 1]),
+            pltpu.make_async_copy(w_down.at[rows, :], chunk_w.at[slot, 0], piece_sem.at[slot, 2]),
+            pltpu.make_async_copy(w_in.at[rows, :], chunk_w.at[slot, 1], piece_sem.at[slot, 3]),
+        ]
+
     act_loads = [
-        pltpu.make_async_copy(src, act.at[i], act_sem.at[i]) for i, src in enumerate((query, key, value, grad_mixed))
+        pltpu.make_async_copy(src, act.at[i], act_sem.at[i]) for i, src in enumerate((query, key, value, mixed))
     ]
-    w_loads = [pltpu.make_async_copy(src, weights.at[i], w_sem.at[i]) for i, src in enumerate((w_query, w_key, w_value))]
-    for load in act_loads:
+    w_loads = [
+        pltpu.make_async_copy(src, weights.at[i % 2], w_sem.at[i])
+        for i, src in enumerate((w_out, w_query, w_key, w_value))
+    ]
+    grad_ffn, first_low, resid_low = act.at[2], grads.at[1], act.at[3]
+    f_loads = [
+        pltpu.make_async_copy(src, dst, f_sem.at[i])
+        for i, (src, dst) in enumerate(
+            ((grad_ffn_in, grad_ffn), (first_low_in, first_low), (second, acc), (first_in, before), (resid_in, resid_low))
+        )
+    ]
+    for load in f_loads[:1] + chunk_loads(0) + f_loads[1:4] + [act_loads[3], w_loads[0], w_loads[1]]:
         load.start()
     barrier = pltpu.get_barrier_semaphore()
     for peer in [core, across, side] + others:
@@ -379,43 +402,35 @@
     hs = slab // 2
     ps = hs // nz
     rs = min(ps, 32)
-    given = sum(heights)
-    full = given // slab
-
-    row = 0
-    ahead = 5
-    issues = []
-    for term, height in zip(terms, heights):
-        step = min(height, slab)
-        for off in range(0, height, step):
-            issues.append((term, off, (row + off) // slab, (row + off) % slab, step))
-        row += height
-
-    def issue(term, off, k, at, step):
-        rows, place = pl.ds(off, step), pl.ds(at, step)
-        remote(term.at[:, 1 - c, rows, :], core_in.at[k, :, place, :], c_s.at[k], c_r.at[k], core).start()
-        sem = load_sem.at[k] if not isinstance(k, int) or k < full else load_sem.at[count]
-        pltpu.make_async_copy(term.at[:, c, rows, :], own.at[k, :, place, :], sem).start()
-
-    upfront = slab > own_heights
-    for k, entry in enumerate(issues):
-        if upfront or k < ahead:
-            issue(*entry)
-
-    def issue_later(k):
-        start = 0
-        for term, height in zip(terms, heights):
-            first, last = start // slab, (start + height) // slab
-
-            @pl.when((k >= first) & (k < last))
-            def _():
-                off = pl.multiple_of((k - first) * slab, slab)
-                issue(term, off, k, 0, slab)
-
-            start += height
-
-    for load in w_loads:
-        load.start()
+    given = 2 * share
+
+    def slab_of(mat, group, sub):
+        if fine:
+            return (group * 2 * subs + mat * subs if mat is not None else group * subs + given // slab) + sub, 0
+        if mat is not None:
+            return mat, pl.multiple_of(group * tile, tile)
+        return given // slab, pl.multiple_of(group * tile, tile)
+
+    def deliver(mat, group, lane, p, mine, value):
+        @pl.when(jnp.logical_not(mine))
+        def _():
+            act[lane, pl.ds(pl.multiple_of(p * tile, tile), tile), :] = value
+            for sub in range(subs):
+                k, at = slab_of(mat, group, sub)
+                src = act.at[lane, pl.ds(pl.multiple_of(p * tile + sub * part, part), part), :]
+                remote(src, core_in.at[k, p, pl.ds(at, part), :], c_s.at[k], c_r.at[k], core).start()
+
+        @pl.when(mine)
+        def _():
+            for sub in range(subs):
+                k, at = slab_of(mat, group, sub)
+                own[k, p, pl.ds(at, part)] = value[sub * part : (sub + 1) * part]
+
+    def sent(mat, group):
+        for sub in range(subs):
+            k, at = slab_of(mat, group, sub)
+            rows = core_in.at[k, :, pl.ds(at, part), :]
+            remote(rows, rows, c_s.at[k], c_r.at[k], core).wait_send()
 
     def core_copy(k):
         return remote(core_in.at[k], core_in.at[k], c_s.at[k], c_r.at[k], core)
@@ -440,14 +455,14 @@
         return remote(mine, mine, xg_s.at[k], xg_r.at[k], side)
 
     def out_copy(k):
-        rows = pl.ds(pl.multiple_of(k * slab, slab), slab)
+        start = k * slab
+        if fine:
+            mat, rest = lax.rem(lax.div(k, subs), 2), lax.div(k, 2 * subs) * tile + lax.rem(k, subs) * slab
+            start = jnp.where(k < given // slab, mat * share + rest, start)
+        rows = pl.ds(pl.multiple_of(start, slab), slab)
         return pltpu.make_async_copy(own.at[k, 1 - y], out.at[rows, :], out_sem.at[k])
 
     def stage_core(k):
-        @pl.when(k < full)
-        def _():
-            pltpu.make_async_copy(own.at[k], own.at[k], load_sem.at[k]).wait()
-
         core_copy(k).wait_recv()
 
         def add(r):
@@ -536,34 +551,121 @@
         v_own[0:1, cols] = jnp.sum(grad_q.astype(f32), axis=0, keepdims=True)
         v_own[1:2, cols] = jnp.sum(grad_v.astype(f32), axis=0, keepdims=True)
 
-    def term(m):
-        step = min(own_heights, slab)
-        for cc, mine in ((1 - c, False), (c, True)):
-            for p in range(2):
-                left = resid_t[pl.ds(pl.multiple_of((p * 2 + cc) * own_heights, own_heights), own_heights), :]
-                tile = dot(left, grads[m], ((1,), (0,))).astype(bf16)
-                if not mine:
-                    act[m, p * own_heights : (p + 1) * own_heights] = tile
-                for off in range(0, own_heights, step):
-                    start = given + m * own_heights + off
-                    k, at = lax.div(start, slab), pl.multiple_of(lax.rem(start, slab), step)
-                    if mine:
-                        own[k, p, pl.ds(at, step)] = tile[off : off + step]
-                    else:
-                        src = act.at[m, pl.ds(p * own_heights + off, step), :]
-                        dst = core_in.at[k, p, pl.ds(at, step), :]
-                        remote(src, dst, c_s.at[k], c_r.at[k], core).start()
-
-    blocks = 4
-    block = slots // blocks
-
-    def resid_rows(r):
-        rows = pl.ds(pl.multiple_of(r * block, block), block)
-        total = grad_first[rows, :]
-        for m in range(3):
-            total += dot(grads[m, rows, :], weights[m], ((1,), (1,)))
-        grad_tokens[rows, :] = total.astype(bf16)
-        time_sum[...] += jnp.sum(total, axis=0, keepdims=True)
+    def feed_chunk(u):
+        group, i, slot = lax.div(u, 4), lax.rem(u, 4), lax.rem(u, 2)
+
+        @pl.when((i == 0) & (group > 0))
+        def _():
+            sent(0, group - 1)
+            sent(1, group - 1)
+
+        for load in chunk_loads(u):
+            load.wait()
+
+        @pl.when(u == 0)
+        def _():
+            for load in f_loads[:3]:
+                load.wait()
+
+        @pl.when(u + 1 < 4 * groups)
+        def _():
+            for load in chunk_loads(u + 1):
+                load.start()
+
+        mine, p, shard = i >= 2, lax.rem(i, 2), shard_of(i)
+        grad_hidden = dot(grad_ffn[...], chunk_w[slot, 0], ((1,), (1,)))
+        grad_pre = (grad_hidden * pieces[slot, 1].astype(f32)).astype(bf16)
+        cols = pl.ds(pl.multiple_of(group * tile, tile), tile)
+        v_own[pl.ds(8 + shard, 1), cols] = jnp.sum(grad_pre.astype(f32), axis=0, keepdims=True)
+        deliver(0, group, 0, p, mine, dot(pieces[slot, 0], grad_ffn[...], ((0,), (0,))).astype(bf16))
+        deliver(1, group, 1, p, mine, dot(grad_pre, first_low[...], ((0,), (0,))).astype(bf16))
+
+        acc[...] += dot(grad_pre, chunk_w[slot, 1], ((1,), (0,)))
+
+    def norm_backward():
+        sent(0, groups - 1)
+        sent(1, groups - 1)
+        for load in act_loads[:3]:
+            load.start()
+        f_loads[3].wait()
+        v_own[2:3, :] = jnp.zeros((1, width), f32)
+        v_own[4:6, :] = jnp.zeros((2, width), f32)
+
+        def rows_of(r):
+            grad, value = acc[r, :], before[r, :]
+            center = value - jnp.mean(value, axis=-1, keepdims=True)
+            spread = lax.rsqrt(jnp.mean(center * center, axis=-1, keepdims=True) + norm_eps)
+            xhat = center * spread
+            scaled = grad * gain[...]
+            inner = scaled - jnp.mean(scaled, axis=-1, keepdims=True)
+            result = spread * (inner - xhat * jnp.mean(scaled * xhat, axis=-1, keepdims=True))
+            low = result.astype(bf16)
+            acc[r, :] = result
+            grads[2, r, :] = low
+            v_own[2:3, :] += jnp.sum(low.astype(f32), axis=0, keepdims=True)
+            v_own[4:5, :] += jnp.sum(grad * xhat, axis=0, keepdims=True)
+            v_own[5:6, :] += jnp.sum(grad, axis=0, keepdims=True)
+
+        _row_loop(slots, 32, rows_of)
+
+    def term(m, left, right):
+        def run(i, carry):
+            rows = pl.ds(pl.multiple_of(shard_of(i) * tile, tile), tile)
+            value = dot(left[:, rows], right[...], ((0,), (0,))).astype(bf16)
+            deliver(None, m, m - 1 if not isinstance(m, int) or m else 0, lax.rem(i, 2), i >= 2, value)
+            return carry
+
+        lax.fori_loop(0, 4, run, 0)
+
+    def out_backward():
+        act_loads[3].wait()
+        w_loads[0].wait()
+        deliver_lane = grads.at[0]
+
+        def run(i, carry):
+            rows = pl.ds(pl.multiple_of(shard_of(i) * tile, tile), tile)
+            value = dot(act[3, :, rows], grads[2], ((0,), (0,))).astype(bf16)
+            p = lax.rem(i, 2)
+
+            @pl.when(i < 2)
+            def _():
+                deliver_lane[pl.ds(pl.multiple_of(p * tile, tile), tile), :] = value
+                for sub in range(subs):
+                    k, at = slab_of(None, 0, sub)
+                    src = deliver_lane.at[pl.ds(pl.multiple_of(p * tile + sub * part, part), part), :]
+                    remote(src, core_in.at[k, p, pl.ds(at, part), :], c_s.at[k], c_r.at[k], core).start()
+
+            @pl.when(i >= 2)
+            def _():
+                for sub in range(subs):
+                    k, at = slab_of(None, 0, sub)
+                    own[k, p, pl.ds(at, part)] = value[sub * part : (sub + 1) * part]
+
+            return carry
+
+        lax.fori_loop(0, 4, run, 0)
+
+        def mix(r):
+            act[3, r, :] = dot(grads[2, r, :], weights[0], ((1,), (1,))).astype(bf16)
+
+        _row_loop(slots, 128, mix)
+        w_loads[2].start()
+        sent(None, 0)
+
+    def resid_part(m):
+        w_loads[m + 1].wait()
+
+        def rows_of(r):
+            value = acc[r, :] + dot(grads[m, r, :], weights[(m + 1) % 2], ((1,), (1,)))
+            if m < 2:
+                acc[r, :] = value
+            else:
+                grad_tokens[r, :] = value.astype(bf16)
+                time_sum[...] += jnp.sum(value, axis=0, keepdims=True)
+
+        _row_loop(slots, 128, rows_of)
+        if m == 0:
+            w_loads[3].start()
 
     v_half = v_core.shape[0]
     v_mine = pl.ds(pl.multiple_of(c * v_half, v_half), v_half)
@@ -632,51 +734,83 @@
             w_copy(q, 1 + nz).wait_recv()
 
     stages = [stage_y, stage_x, stage_z, stage_zg, stage_xg]
-    n_units = pairs + 3 + blocks
-    base = 0 if slab <= own_heights else pairs + 4
-    small = [(pairs + at, functools.partial(v_stage, i)) for i, at in enumerate((0, 2, 5, 7, 9, 10))]
-    for q, first in ((0, 0), (1, n_units)):
+    feed = 4 * groups
+    per = 2 * subs
+    terms_at = feed + 4
+    base = 4 if fine else terms_at + 3
+    small = [(feed + 4 + at, functools.partial(v_stage, i)) for i, at in enumerate((0, 1, 4, 6, 8, 9))]
+    for q, first in ((0, 2), (1, terms_at + 6)):
         small += [(first + at, functools.partial(w_stage, q, i)) for i, at in enumerate((0, 3, 5, 7, 8))]
     ticks = max([base + count + lag * (len(stages) - 1)] + [at + 1 for at, _ in small])
     v_own[...] = vec[...]
     time_sum[...] = jnp.zeros_like(time_sum)
-    for load in act_loads:
-        load.wait()
+
+    def cores(start, stop):
+        def run(k, carry):
+            stage_core(k)
+            return carry
+
+        lax.fori_loop(start, stop, run, 0)
 
     def tick(t, carry):
-        @pl.when(t < pairs)
+        @pl.when(t < feed)
         def _():
-            head_pair(t)
-
-        @pl.when((t >= pairs) & (t < pairs + 3))
+            feed_chunk(t)
+
+        @pl.when(t == feed)
         def _():
-            term(t - pairs)
-
-        @pl.when(t == pairs + 3)
+            norm_backward()
+
+        @pl.when(t == feed + 1)
         def _():
-            for load in w_loads:
+            out_backward()
+            for load in act_loads[:3]:
                 load.wait()
 
-        @pl.when((t >= pairs + 3) & (t < n_units))
+        @pl.when((t > feed) & (t < terms_at))
         def _():
-            resid_rows(t - pairs - 3)
-
-        if row > full * slab:
-
-            @pl.when(t == base)
+            done = 3 * (t - feed - 1)
+
+            def run(p, carry):
+                head_pair(p)
+                return carry
+
+            lax.fori_loop(done, jnp.minimum(done + 3, pairs), run, 0)
+
+        @pl.when((t >= terms_at) & (t < terms_at + 3))
+        def _():
+            m = t - terms_at
+
+            @pl.when(m == 0)
             def _():
-                part = own.at[full, :, pl.ds(0, row - full * slab), :]
-                pltpu.make_async_copy(part, part, load_sem.at[count]).wait()
-
-        if not upfront:
-            issue_later(t - base + ahead)
-
-        for i in range(3):
-            k = t - base + i
-
-            @pl.when((k < count) & ((t == base) | ((t > base) & (i == 2))))
+                f_loads[4].start()
+                f_loads[4].wait()
+
+            term(m + 1, resid_low, grads.at[m])
+
+        for m in range(3):
+
+            @pl.when(t == terms_at + 3 + m)
             def _():
-                stage_core(k)
+                resid_part(m)
+
+        if fine:
+
+            @pl.when((t < feed) & (lax.rem(t, 4) == 3))
+            def _():
+                start = lax.div(t, 4) * per
+                cores(start, start + per)
+
+            @pl.when((t == feed + 1) | ((t >= terms_at) & (t < terms_at + 3)))
+            def _():
+                start = given // slab + jnp.maximum(t - terms_at + 1, 0) * subs
+                cores(start, start + subs)
+
+        else:
+
+            @pl.when(t == terms_at + 2)
+            def _():
+                cores(0, count)
 
         for d, stage in enumerate(stages):
             k = t - base - d * lag
@@ -691,9 +825,10 @@
         return carry
 
     lax.fori_loop(0, ticks, tick, 0)
+    for m in range(3):
+        sent(None, m + 1)
 
     def finish(k, carry):
-        core_copy(k).wait_send()
         x_copy(k).wait_send()
         for o in range(1, nz):
             z_copy(k, o).wait_send()
@@ -710,27 +845,28 @@
             w_copy(q, i).wait_send()
 
 
-def attend_and_reduce(dp_n, terms, acts, weights, log_total, keep, resid_t, grad_first, vec, embed):
-    slots, width = acts[0].shape
-    heights = tuple(t.shape[2] for t in terms)
-    own_heights = width // 4
-    rows = sum(heights) + 3 * own_heights
+def backward_and_reduce(dp_n, streams, inside_args):
+    slots, units = streams[0].shape
+    vec, embed = inside_args[-2:]
+    width = vec.shape[1]
+    tile = width // 4
+    rows = 2 * units // 4 + 4 * tile
     slab = max(128, 16 * dp_n)
     count, nz = rows // slab, dp_n // 2
     bf16, f32 = jnp.bfloat16, jnp.float32
     dma, vmem = pltpu.SemaphoreType.DMA, pltpu.VMEM
     v_shape = vec.shape
+    half_shape = (v_shape[0] // 2, width)
     anywhere, inside = pl.BlockSpec(memory_space=pl.ANY), pl.BlockSpec(memory_space=pltpu.VMEM)
-    half_shape = (v_shape[0] // 2, width)
     return pl.pallas_call(
-        functools.partial(_backward_kernel, dp_n, slab, 1, heights, own_heights),
+        functools.partial(_backward_kernel, dp_n, slab, 1),
         out_shape=[
             jax.ShapeDtypeStruct((rows, width), bf16),
             jax.ShapeDtypeStruct(v_shape, f32),
             jax.ShapeDtypeStruct((2, dp_n, 2, 2) + embed.shape, f32),
             jax.ShapeDtypeStruct((slots, width), bf16),
         ],
-        in_specs=[anywhere] * (len(terms) + 7) + [inside] * 6,
+        in_specs=[anywhere] * len(streams) + [inside] * len(inside_args),
         out_specs=[anywhere, inside, inside, inside],
         scratch_shapes=[
             vmem((count, 2, slab, width), bf16),
@@ -740,7 +876,11 @@
             vmem((count, nz, slab // 2 // nz, width), bf16),
             vmem((4, slots, width), bf16),
             vmem((3, slots, width), bf16),
-            vmem((3, width, width), bf16),
+            vmem((2, width, width), bf16),
+            vmem((2, 2, slots, tile), bf16),
+            vmem((2, 2, tile, width), bf16),
+            vmem((slots, width), f32),
+            vmem((slots, width), f32),
             vmem((1, width), f32),
             vmem(v_shape, f32),
             vmem(half_shape, f32),
@@ -749,15 +889,15 @@
             vmem((nz,) + half_shape, f32),
             vmem((3,) + half_shape, f32),
         ]
-        + [dma((count + 1,)), dma((4,)), dma((3,))]
+        + [dma((2, 4)), dma((4,)), dma((4,)), dma((5,))]
         + [dma((count,))] * 6
         + [dma((count, nz))] * 4
         + [dma((count,))] * 3
         + [dma((3 + nz,))] * 2
         + [dma((2, 2 + nz))] * 2,
-        compiler_params=pltpu.CompilerParams(collective_id=1, has_side_effects=True, vmem_limit_bytes=66_000_000),
-        name="attend_and_reduce",
-    )(*terms, *acts, *weights, log_total, keep, resid_t, grad_first, vec, embed)
+        compiler_params=pltpu.CompilerParams(collective_id=1, has_side_effects=True, vmem_limit_bytes=67_043_328),
+        name="backward_and_reduce",
+    )(*streams, *inside_args)
 
 
 def local(
@@ -826,9 +966,7 @@
         b_in.astype(f32).reshape(1, -1),
         row_keep,
     )
-    first_norm, first_pull = jax.vjp(
-        layer_norm, first_in, gain_one.astype(f32), shift_one.astype(f32)
-    )
+    first_norm = layer_norm(first_in, gain_one.astype(f32), shift_one.astype(f32))
     first_low = first_norm.astype(bf16)
     second_norm, second_pull = jax.vjp(
         layer_norm, first_norm + ffn_out, gain_two.astype(f32), shift_two.astype(f32)
@@ -836,45 +974,48 @@
     layer_out = (second_norm * row_keep).astype(bf16)
     grad_second_in, grad_gain_two, grad_shift_two = second_pull(cotangent.astype(f32) * row_keep)
     grad_ffn = grad_second_in.astype(bf16)
-    grad_hidden = mm(grad_ffn, full_down, ((1,), (1,)))
-    grad_pre = (grad_hidden * gelu_slope).astype(bf16)
-    grad_first = grad_second_in + mm(grad_pre, full_in, ((1,), (0,)))
-    term_in = mm(grad_pre, first_low, ((0,), (0,))).astype(bf16)
-    term_down = mm(hidden_low, grad_ffn, ((0,), (0,))).astype(bf16)
-    grad_first_in, grad_gain_one, grad_shift_one = first_pull(grad_first)
-    grad_attn = grad_first_in.astype(bf16)
-    grad_mixed = mm(grad_attn, full_out, ((1,), (1,))).astype(bf16)
-    terms = [
-        term_down,
-        term_in,
-        mm(mixed_rows, grad_attn, ((0,), (0,))).astype(bf16),
-    ]
-    zero = jnp.zeros((width,), f32)
-    vec = jnp.stack(
+    zero = jnp.zeros((1, width), f32)
+    vec = jnp.concatenate(
         [
             zero,
             zero,
-            jnp.sum(grad_attn, axis=0, dtype=f32),
-            jnp.sum(grad_ffn, axis=0, dtype=f32),
-            grad_gain_one,
-            grad_shift_one,
-            grad_gain_two,
-            grad_shift_two,
+            zero,
+            jnp.sum(grad_ffn, axis=0, dtype=f32, keepdims=True),
+            zero,
+            zero,
+            grad_gain_two[None],
+            grad_shift_two[None],
+            jnp.zeros((-(-b_in.shape[0] // width) // 8 * 8 + 8, width), f32),
         ]
     )
-    vec = jnp.concatenate([vec, jnp.sum(grad_pre, axis=0, dtype=f32).reshape(-1, width)], axis=0)
-    vec = jnp.pad(vec, ((0, -vec.shape[0] % 8), (0, 0)))
-    sums, vectors, every, grad_tokens = attend_and_reduce(
+    sums, vectors, every, grad_tokens = backward_and_reduce(
         dp_n,
-        [t.reshape(2, 2, -1, width) for t in terms],
-        [query_rows, key_rows, value_rows, grad_mixed],
-        [full_query, full_key, full_value],
-        log_total,
-        row_keep,
-        resid_low.T,
-        grad_first_in,
-        vec,
-        time_embed.astype(f32).reshape(-1, 128),
+        [
+            hidden_low,
+            gelu_slope,
+            full_down,
+            full_in,
+            grad_second_in,
+            first_in,
+            query_rows,
+            key_rows,
+            value_rows,
+            mixed_rows,
+            full_out,
+            full_query,
+            full_key,
+            full_value,
+            grad_ffn,
+            first_low,
+            resid_low,
+        ],
+        [
+            log_total,
+            row_keep,
+            gain_one.astype(f32).reshape(1, -1),
+            vec,
+            time_embed.astype(f32).reshape(-1, 128),
+        ],
     )
     time_rows, time_grads = every.reshape(2, -1, width).astype(bf16)
     own_columns = lax.dynamic_slice_in_dim(time_rows, seq_rank * rows, rows, 1)
@@ -882,7 +1023,7 @@
     grad_b_time = jnp.sum(time_grads, axis=0, dtype=f32)
     grad_b_in = vectors[8 : 8 + b_in.shape[0] // width].reshape(-1)
     sums = sums.astype(f32)
-    down_rows, in_rows = (t.shape[0] // 4 for t in terms[:2])
+    down_rows = in_rows = w_in.shape[0]
     ends = [0, down_rows, down_rows + in_rows]
     ends += [ends[-1] + rows * i for i in range(1, 5)]
     share_down, share_in, share_out, share_q, share_k, share_v = (

time: 358 us -> 345 us (0.964)
  matrix products: 40.9 us -> 1.29 us
  Pallas kernels: 278 us -> 300 us
  other arithmetic: 13.5 us -> 17.5 us
    dot_general x7 -> x1, matrix products: 40.9 us -> 1.29 us  [mm(): return lax.dot_general(a, b, (dims, ((), ())), preferred_element_type=f32)]
    pallas_call x1, Pallas kernels: 179 us -> 201 us  [backward_and_reduce(): pl.pallas_call(functools.partial(_backward_kernel, dp_n, slab, 1), out_sh...]
where the time goes in v1:
time: 345 us; the launch traced here: 344 us
  Pallas kernels  300 us (87%)
  local copies, waits for them, and re-layouts  23.7 us (7%)
  other arithmetic  17.5 us (5%)
    pallas_call x1, Pallas kernels, backward_and_reduce(): pl.pallas_call(functools.partial(_backward_kernel, dp_n, slab, 1), out_sh...  201 us
    pallas_call x1, Pallas kernels, gather_and_forward(): pl.pallas_call(functools.partial(_forward_kernel, sizes), out_shape=[jax....  98.9 us
    slice x2, local copies, waits for them, and re-layouts, local(): sums[lo:hi]  8.34 us

profile of v1, /device:TPU:0, one launch (start us, length us, event | category | flops | bytes accessed | tf_op | source)
XLA Modules:
  0.0 343.8 jit_solution(6022083390631275084)
XLA Ops:
  0.7 1.2 dynamic_slice.8
  2.6 0.7 convert_element_type.52
  3.3 0.7 convert_element_type.50
  3.9 0.0 copy-start.5
  3.9 0.7 stack.26
  4.6 0.7 stack.27
  5.3 0.7 stack.28
  6.0 0.7 stack.25
  6.7 0.7 stack.31
  7.4 0.7 convert_element_type.53
  8.1 0.7 stack.29
  8.7 0.7 convert_element_type.51
  9.4 0.7 stack.30
  10.1 0.1 stack.32
  10.2 1.4 fusion.20
  11.5 0.6 convert_element_type.48.refs_9_
  12.2 1.3 reshape.137
  13.5 0.6 broadcast_in_dim.15.refs_8_
  14.1 0.7 fusion.4.refs_11_.refs_18_
  14.8 98.9 %gather_and_forward.1 = (bf16[1024,1024]{1,0:T(8,128)(2,1)}, bf16[1024,1024]{1,0:T(8,128)(2,1)}, bf16[1024,1024]{1,0:T(8,128)(2,1)}, bf16[1024,1024]{1,0:T(8,128...) custom-call(bf16[256,1024]{1,0:T(8,128)(2,1)} %refs_0_.1, ...), custom_call_target="tpu_custom_call" | custom-call | tf_op jit(solution)/shard_map/gather_and_forward/pallas_call | solution.py:301
  113.7 0.0 copy-start
  113.7 1.9 reduce_sum.86
  115.7 0.0 copy-start.3
  115.7 0.3 copy-done
  116.0 0.3 multiply_reduce_fusion.3
  116.3 0.0 copy-done.5
  116.3 1.0 copy-done.3
  117.3 1.6 fusion.14
  118.9 0.0 copy-start.2
  118.9 0.3 multiply_reduce_fusion.2
  119.3 0.9 copy-done.2
  120.2 0.9 multiply_reduce_fusion
  121.1 2.0 fusion.13
  123.2 1.9 convert_reduce_fusion
  125.1 1.3 concatenate.11.refs_20_
  126.4 200.9 %backward_and_reduce.1 = (bf16[3072,1024]{1,0:T(8,128)(2,1)}, f32[16,1024]{1,0:T(8,128)}, f32[2,8,2,2,8,128]{5,4,3,2,1,0:T(8,128)}, bf16[512,1024]{1,0:T(8,128)(2,1)}) custom-call(bf16[512,4096]{1,0:T(8,128)(2,1)} %get-tuple-element.41.refs_0_, bf16[512,4096]{1,0:T(8,128)(2,1)} %get-tuple-element.42.refs_1_, bf16[4096,1024]{1,0:T(8,128)(2,1)} %get-tuple-element.43.refs_2_, ...), custom_call_target="tpu_custom_call" | custom-call | tf_op jit(solution)/shard_map/backward_and_reduce/pallas_call | solution.py:861
  327.3 0.8 slice_bitcast_fusion
  328.0 1.8 fusion.19
  329.9 0.6 copy.48
  330.5 1.0 convert_element_type.61
  331.5 0.6 convert_reduce_fusion.1
  332.1 1.3 fusion.5
  333.4 0.0 copy-start.1
  333.4 3.9 %fusion.17 = (f32[256,1024]{1,0:T(8,128)}, f32[256,1024]{1,0:T(8,128)}, f32[256,1024]{1,0:T(8,128)}, f32[256,1024]{1,0:T(8,128)}) fusion(bf16[3072,1024]{1,0:T(8,128)(2,1)} %get-tuple-element.56), kind=kLoop, calls=%fused_computation.37 | loop fusion | bytes 8388608 | tf_op jit(solution)/shard_map/slice | solution.py:1030
  337.3 1.0 copy-done.1
  338.4 0.0 copy-start.4
  338.4 4.4 %fusion.16 = (f32[1024,1024]{1,0:T(8,128)}, f32[1024,1024]{1,0:T(8,128)}) fusion(bf16[3072,1024]{1,0:T(8,128)(2,1)S(1)} %copy-done.1), kind=kLoop, calls=%fused_computation.36 | loop fusion | bytes 16777216 | tf_op jit(solution)/shard_map/slice | solution.py:1030
  342.8 0.0 copy-done.4
  342.8 1.0 copy.50
  (12 shorter events, 0.1 us)
Async XLA Ops:
  3.9 112.4 %copy-start.5 = (f32[1024]{0:T(1024)}, f32[1024]{0:T(1024)S(1)}, u32[]{:S(2)}) copy-start(f32[1024]{0:T(1024)S(1)} %convert_element_type.50) | copy-start | bytes 12292
  113.7 2.2 copy-start
  115.7 1.7 copy-start.3
  118.9 1.2 copy-start.2
  333.4 4.9 %copy-start.1 = (bf16[3072,1024]{1,0:T(8,128)(2,1)S(1)}, bf16[3072,1024]{1,0:T(8,128)(2,1)}, u32[]{:S(2)}) copy-start(bf16[3072,1024]{1,0:T(8,128)(2,1)} %get-tuple-element.56) | copy-start | bytes 18874372
  338.4 4.4 %copy-start.4 = (bf16[512,1024]{1,0:T(8,128)(2,1)S(1)}, bf16[512,1024]{1,0:T(8,128)(2,1)}, u32[]{:S(2)}) copy-start(bf16[512,1024]{1,0:T(8,128)(2,1)} %get-tuple-element.109) | copy-start | bytes 3145732

commit v2 on v1

--- a/solution.py
+++ b/solution.py
@@ -30,15 +30,15 @@
 
 def _forward_kernel(sizes, *refs):
     n = len(sizes)
-    given, (tokens, embed, rows_in, bias_in, keep) = refs[:n], refs[n : n + 5]
-    outs = refs[n + 5 : 2 * n + 5]
-    (resid_out, query_out, key_out, value_out, mixed_out, pre_out, hidden_out, slope_out, ffn_out, log_total) = refs[
-        2 * n + 5 : 2 * n + 15
-    ]
-    full = refs[2 * n + 15 : 3 * n + 15]
-    act, pre, first_low, hidden, slope, total = refs[3 * n + 15 : 3 * n + 21]
+    given, (tokens, embed, cotangent, lengths) = refs[:n], refs[n : n + 4]
+    biases, refs = refs[n + 4 : n + 14], refs[n + 14 :]
+    outs = refs[:n]
+    (resid_out, query_out, key_out, value_out, mixed_out, pre_out, hidden_out, slope_out, second_out) = refs[n : n + 9]
+    grad_out, first_out, log_total, layer_out, vec = refs[n + 9 : n + 14]
+    full = refs[n + 14 : 2 * n + 14]
+    act, pre, first_low, hidden, slope, total, rows_in, bias_in = refs[2 * n + 14 : 2 * n + 22]
     load_sem, save_sem, act_sem, c_send, c_recv, y_send, y_recv, x_send, x_recv, f_send, f_recv, g_send, g_recv = refs[
-        3 * n + 21 :
+        2 * n + 22 :
     ]
     f32, bf16 = jnp.float32, jnp.bfloat16
     w_time, w_query, w_key, w_value, w_out, w_in, w_down = full
@@ -127,6 +127,11 @@
     def dot(a, b, dims):
         return lax.dot_general(a, b, (dims, ((), ())), preferred_element_type=f32)
 
+    for i, ref in enumerate(biases[:9]):
+        rows_in[i : i + 1, :] = ref[...].astype(f32).reshape(1, width)
+    bias_in[...] = biases[9][...].astype(f32).reshape(bias_in.shape)
+    bound = lengths[me] + BLOCK
+
     def bias(i):
         return rows_in[i : i + 1, :]
 
@@ -153,7 +158,8 @@
     step(1)
     turn(0)
     complete(0)
-    time_proj = dot(embed[...], w_time[...], ((1,), (0,)))[0:1] + bias(0)
+    wide = jnp.broadcast_to(embed[...].astype(f32), (16, width)).astype(bf16)
+    time_proj = dot(wide, w_time[...], ((1,), (0,)))[0:1] + bias(0)
 
     def enter(r):
         value = tokens[r, :].astype(f32) + time_proj
@@ -161,7 +167,7 @@
         act[0, r, :] = value.astype(bf16)
 
     tiles(slots, 64, enter)
-    save(act.at[0], resid_out, act_sem.at[0])
+    pltpu.make_async_copy(act.at[0], resid_out, act_sem.at[0]).start()
     for j, (weight, row) in enumerate(((w_query, 1), (w_key, None), (w_value, 2))):
         step(j + 2)
         turn(j + 1)
@@ -173,7 +179,7 @@
     def head_pair(p):
         cols = pl.ds(pl.multiple_of(p * pair, pair), pair)
         q2, k2, v2 = (act[i, :, cols] for i in (1, 2, 3))
-        kept = keep[...] > 0
+        kept = lax.broadcasted_iota(jnp.int32, (slots, 1), 0) < bound
         found = []
         for h in range(2):
             mask = jnp.where(first == (h == 0), scale, 0.0)
@@ -218,6 +224,7 @@
         first_low[r, :] = layer_norm(pre[r, :], bias(4), bias(5)).astype(bf16)
 
     tiles(slots, 32, norm_rows)
+    save(first_low, first_out, act_sem.at[10])
 
     def feed_up(start, size):
         rows = pl.ds(pl.multiple_of(start, size), size)
@@ -278,7 +285,32 @@
         arrived(j)
     save(w_down, outs[6], save_sem.at[6])
     down_shards((me ^ 2, me ^ 3), False)
-    save(total, ffn_out, act_sem.at[8])
+    pltpu.make_async_copy(act.at[0], resid_out, act_sem.at[0]).wait()
+    vec[...] = jnp.zeros_like(vec)
+
+    def second_rows(r):
+        first_norm = layer_norm(pre[r, :], bias(4), bias(5))
+        value = first_norm + total[r, :]
+        center = value - jnp.mean(value, axis=-1, keepdims=True)
+        spread = lax.rsqrt(jnp.mean(center * center, axis=-1, keepdims=True) + norm_eps)
+        xhat = center * spread
+        rows = r.start + lax.broadcasted_iota(jnp.int32, (r.size, 1), 0)
+        valid = jnp.where(rows < bound, 1.0, 0.0)
+        layer_out[r, :] = ((xhat * bias(7) + bias(8)) * valid).astype(bf16)
+        grad = cotangent[r, :].astype(f32) * valid
+        scaled = grad * bias(7)
+        inner = scaled - jnp.mean(scaled, axis=-1, keepdims=True)
+        result = spread * (inner - xhat * jnp.mean(scaled * xhat, axis=-1, keepdims=True))
+        low = result.astype(bf16)
+        total[r, :] = result
+        act[0, r, :] = low
+        vec[3:4, :] += jnp.sum(low.astype(f32), axis=0, keepdims=True)
+        vec[6:7, :] += jnp.sum(grad * xhat, axis=0, keepdims=True)
+        vec[7:8, :] += jnp.sum(grad, axis=0, keepdims=True)
+
+    tiles(slots, 32, second_rows)
+    save(total, second_out, act_sem.at[8])
+    save(act.at[0], grad_out, act_sem.at[9])
     for copy in saves:
         copy.wait()
     for a in range(n):
@@ -288,7 +320,7 @@
             copy(j).wait_send()
 
 
-def gather_and_forward(arrays, tokens, embed, rows_in, bias_in, keep):
+def gather_and_forward(arrays, tokens, embed, cotangent, lengths, biases):
     sizes = tuple(a.shape[0] for a in arrays)
     n = len(arrays)
     m = sum(max(1, r // 256) for r in sizes)
@@ -298,15 +330,24 @@
     dma, vmem = pltpu.SemaphoreType.DMA, pltpu.VMEM
     anywhere, inside = pl.BlockSpec(memory_space=pl.ANY), pl.BlockSpec(memory_space=pltpu.VMEM)
     wide = jax.ShapeDtypeStruct((slots, width), bf16)
+    wide_f32 = jax.ShapeDtypeStruct((slots, width), f32)
     return pl.pallas_call(
         functools.partial(_forward_kernel, sizes),
         out_shape=[jax.ShapeDtypeStruct((4 * a.shape[0], a.shape[1]), a.dtype) for a in arrays]
         + [wide] * 5
-        + [jax.ShapeDtypeStruct((slots, width), f32)]
+        + [wide_f32]
         + [jax.ShapeDtypeStruct((slots, units), bf16)] * 2
-        + [jax.ShapeDtypeStruct((slots, width), f32), jax.ShapeDtypeStruct((width // HEAD_DIM, slots), f32)],
-        in_specs=[anywhere] * n + [inside] * 5,
-        out_specs=[anywhere] * (n + 9) + [inside],
+        + [wide_f32, wide, wide]
+        + [
+            jax.ShapeDtypeStruct((width // HEAD_DIM, slots), f32),
+            wide,
+            jax.ShapeDtypeStruct((8 + units // width + -units // width % 8, width), f32),
+        ],
+        in_specs=[anywhere] * n
+        + [inside] * 3
+        + [pl.BlockSpec(memory_space=pltpu.SMEM)]
+        + [inside] * len(biases),
+        out_specs=[anywhere] * (n + 11) + [inside] * 3,
         scratch_shapes=[vmem((4 * a.shape[0], a.shape[1]), a.dtype) for a in arrays]
         + [
             vmem((5, slots, width), bf16),
@@ -315,15 +356,17 @@
             vmem((slots, units), bf16),
             vmem((slots, units), bf16),
             vmem((slots, width), f32),
+            vmem((16, width), f32),
+            vmem((1, units), f32),
         ]
-        + [dma((n,)), dma((n,)), dma((9,))]
+        + [dma((n,)), dma((n,)), dma((11,))]
         + [dma((n,))] * 2
         + [dma((m,))] * 8,
         compiler_params=pltpu.CompilerParams(
             collective_id=0, has_side_effects=True, vmem_limit_bytes=66_000_000
         ),
         name="gather_and_forward",
-    )(*arrays, tokens, embed, rows_in, bias_in, keep)
+    )(*arrays, tokens, embed, cotangent, lengths, *biases)
 
 
 def _row_loop(rows, step, body):
@@ -336,7 +379,7 @@
 
 def _backward_kernel(dp_n, slab, lag, *refs):
     (hidden, slope, w_down, w_in, second, first_in, query, key, value, mixed, w_out, w_query, w_key, w_value) = refs[:14]
-    (grad_ffn_in, first_low_in, resid_in, log_total, keep, gain, vec, embed) = refs[14:22]
+    (grad_ffn_in, first_low_in, resid_in, log_total, gain_in, vec, embed, lengths) = refs[14:22]
     out, vec_out, rec_out, grad_tokens = refs[22:26]
     (own, core_in, y_in, x_in, z_in, act, grads, weights, pieces, chunk_w, acc, before) = refs[26:38]
     (time_sum, v_own, v_core, v_y, v_x, v_z, v_sum) = refs[38:45]
@@ -523,7 +566,7 @@
         cols = pl.ds(pl.multiple_of(p * pair, pair), pair)
         q2, k2, v2, g2 = (act[i, :, cols] for i in range(4))
         first = lax.broadcasted_iota(jnp.int32, (1, pair), 1) < HEAD_DIM
-        kept = keep[...] > 0
+        kept = lax.broadcasted_iota(jnp.int32, (slots, 1), 0) < bound
         found = []
         for h in range(2):
             mask = jnp.where(first == (h == 0), 1.0, 0.0)
@@ -596,7 +639,7 @@
             center = value - jnp.mean(value, axis=-1, keepdims=True)
             spread = lax.rsqrt(jnp.mean(center * center, axis=-1, keepdims=True) + norm_eps)
             xhat = center * spread
-            scaled = grad * gain[...]
+            scaled = grad * gain_in[...].astype(f32).reshape(1, width)
             inner = scaled - jnp.mean(scaled, axis=-1, keepdims=True)
             result = spread * (inner - xhat * jnp.mean(scaled * xhat, axis=-1, keepdims=True))
             low = result.astype(bf16)
@@ -715,12 +758,12 @@
     def w_stage(q, i):
         if i == 0:
             if q == 0:
-                rec_out[0, dp, y, c] = embed[...]
+                value = embed[...].astype(f32)
             else:
-                rounded = time_sum[...].astype(bf16).astype(f32)
-                lanes = embed.shape[-1]
-                for j in range(width // lanes):
-                    rec_out[1, dp, y, c, j : j + 1, :] = rounded[:, j * lanes : (j + 1) * lanes]
+                value = time_sum[...].astype(bf16).astype(f32)
+            lanes = rec_out.shape[-1]
+            for j in range(width // lanes):
+                rec_out[q, dp, y, c, j : j + 1, :] = value[:, j * lanes : (j + 1) * lanes]
             w_copy(q, 0).start()
         elif i < 3:
             w_copy(q, i - 1).wait_recv()
@@ -742,6 +785,7 @@
     for q, first in ((0, 2), (1, terms_at + 6)):
         small += [(first + at, functools.partial(w_stage, q, i)) for i, at in enumerate((0, 3, 5, 7, 8))]
     ticks = max([base + count + lag * (len(stages) - 1)] + [at + 1 for at, _ in small])
+    bound = lengths[me] + BLOCK
     v_own[...] = vec[...]
     time_sum[...] = jnp.zeros_like(time_sum)
 
@@ -847,7 +891,7 @@
 
 def backward_and_reduce(dp_n, streams, inside_args):
     slots, units = streams[0].shape
-    vec, embed = inside_args[-2:]
+    vec, embed = inside_args[-3:-1]
     width = vec.shape[1]
     tile = width // 4
     rows = 2 * units // 4 + 4 * tile
@@ -863,10 +907,12 @@
         out_shape=[
             jax.ShapeDtypeStruct((rows, width), bf16),
             jax.ShapeDtypeStruct(v_shape, f32),
-            jax.ShapeDtypeStruct((2, dp_n, 2, 2) + embed.shape, f32),
+            jax.ShapeDtypeStruct((2, dp_n, 2, 2, width // 128, 128), f32),
             jax.ShapeDtypeStruct((slots, width), bf16),
         ],
-        in_specs=[anywhere] * len(streams) + [inside] * len(inside_args),
+        in_specs=[anywhere] * len(streams)
+        + [inside] * (len(inside_args) - 1)
+        + [pl.BlockSpec(memory_space=pltpu.SMEM)],
         out_specs=[anywhere, inside, inside, inside],
         scratch_shapes=[
             vmem((count, 2, slab, width), bf16),
@@ -900,6 +946,56 @@
     )(*streams, *inside_args)
 
 
+def _widen_kernel(plan, sums, *refs):
+    outs, (low, high, load_sem, save_sem) = refs[: len(plan)], refs[len(plan) :]
+    step = low.shape[1]
+    blocks = [(out, off) for out, rows in zip(outs, plan) for off in range(0, rows, step)]
+
+    def load(i):
+        return pltpu.make_async_copy(sums.at[pl.ds(i * step, step), :], low.at[i % 4], load_sem.at[i % 4])
+
+    def save(i):
+        out, off = blocks[i]
+        return pltpu.make_async_copy(high.at[i % 4], out.at[pl.ds(off, step), :], save_sem.at[i % 4])
+
+    for i in range(min(3, len(blocks))):
+        load(i).start()
+    for i in range(len(blocks)):
+        load(i).wait()
+        if i + 3 < len(blocks):
+            load(i + 3).start()
+        if i >= 4:
+            save(i - 4).wait()
+
+        def widen(r):
+            high[i % 4, r] = low[i % 4, r].astype(jnp.float32)
+
+        _row_loop(step, 64, widen)
+        save(i).start()
+    for i in range(max(0, len(blocks) - 4), len(blocks)):
+        save(i).wait()
+
+
+def widen(sums, plan):
+    width = sums.shape[1]
+    step = 256
+    anywhere = pl.BlockSpec(memory_space=pl.ANY)
+    return pl.pallas_call(
+        functools.partial(_widen_kernel, plan),
+        out_shape=[jax.ShapeDtypeStruct((rows, width), jnp.float32) for rows in plan],
+        in_specs=[anywhere],
+        out_specs=[anywhere] * len(plan),
+        scratch_shapes=[
+            pltpu.VMEM((4, step, width), jnp.bfloat16),
+            pltpu.VMEM((4, step, width), jnp.float32),
+            pltpu.SemaphoreType.DMA((4,)),
+            pltpu.SemaphoreType.DMA((4,)),
+        ],
+        compiler_params=pltpu.CompilerParams(vmem_limit_bytes=64 << 20),
+        name="widen",
+    )(sums)
+
+
 def local(
     dp_n,
     tokens,
@@ -926,20 +1022,12 @@
 ):
     f32, bf16 = jnp.float32, jnp.bfloat16
     seq_rank = lax.axis_index("seq")
-    item_count = time_embed.shape[0]
-    token_count = tokens.shape[0]
-    slot_count = token_count // item_count
     width = tokens.shape[1]
     rows = w_time.shape[0]
 
     def mm(a, b, dims):
         return lax.dot_general(a, b, (dims, ((), ())), preferred_element_type=f32)
 
-    own_lengths = lax.dynamic_slice_in_dim(lengths, seq_rank * item_count, item_count, 0)
-    slot_index = lax.broadcasted_iota(jnp.int32, (item_count, slot_count), 1)
-    own_valid = slot_index < own_lengths[:, None] + BLOCK
-    row_keep = own_valid.reshape(token_count, 1).astype(f32)
-    rows_in = jnp.stack([b_time, b_query, b_value, b_out, gain_one, shift_one, b_down, b_down]).astype(f32)
     (
         _,
         full_query,
@@ -956,37 +1044,19 @@
         first_in,
         hidden_low,
         gelu_slope,
-        ffn_out,
+        grad_second_in,
+        grad_ffn,
+        first_low,
         log_total,
+        layer_out,
+        vec,
     ) = gather_and_forward(
         [w_time, w_query, w_key, w_value, w_out, w_in, w_down],
         tokens,
-        jnp.broadcast_to(time_embed, (16, width)),
-        rows_in,
-        b_in.astype(f32).reshape(1, -1),
-        row_keep,
-    )
-    first_norm = layer_norm(first_in, gain_one.astype(f32), shift_one.astype(f32))
-    first_low = first_norm.astype(bf16)
-    second_norm, second_pull = jax.vjp(
-        layer_norm, first_norm + ffn_out, gain_two.astype(f32), shift_two.astype(f32)
-    )
-    layer_out = (second_norm * row_keep).astype(bf16)
-    grad_second_in, grad_gain_two, grad_shift_two = second_pull(cotangent.astype(f32) * row_keep)
-    grad_ffn = grad_second_in.astype(bf16)
-    zero = jnp.zeros((1, width), f32)
-    vec = jnp.concatenate(
-        [
-            zero,
-            zero,
-            zero,
-            jnp.sum(grad_ffn, axis=0, dtype=f32, keepdims=True),
-            zero,
-            zero,
-            grad_gain_two[None],
-            grad_shift_two[None],
-            jnp.zeros((-(-b_in.shape[0] // width) // 8 * 8 + 8, width), f32),
-        ]
+        time_embed,
+        cotangent,
+        lengths,
+        [b_time, b_query, b_value, b_out, gain_one, shift_one, b_down, gain_two, shift_two, b_in],
     )
     sums, vectors, every, grad_tokens = backward_and_reduce(
         dp_n,
@@ -1009,25 +1079,15 @@
             first_low,
             resid_low,
         ],
-        [
-            log_total,
-            row_keep,
-            gain_one.astype(f32).reshape(1, -1),
-            vec,
-            time_embed.astype(f32).reshape(-1, 128),
-        ],
+        [log_total, gain_one, vec, time_embed, lengths],
     )
     time_rows, time_grads = every.reshape(2, -1, width).astype(bf16)
     own_columns = lax.dynamic_slice_in_dim(time_rows, seq_rank * rows, rows, 1)
     grad_w_time = mm(own_columns, time_grads, ((0,), (0,)))
     grad_b_time = jnp.sum(time_grads, axis=0, dtype=f32)
     grad_b_in = vectors[8 : 8 + b_in.shape[0] // width].reshape(-1)
-    sums = sums.astype(f32)
-    down_rows = in_rows = w_in.shape[0]
-    ends = [0, down_rows, down_rows + in_rows]
-    ends += [ends[-1] + rows * i for i in range(1, 5)]
-    share_down, share_in, share_out, share_q, share_k, share_v = (
-        sums[lo:hi] for lo, hi in zip(ends[:-1], ends[1:])
+    share_down, share_in, share_out, share_q, share_k, share_v = widen(
+        sums, (w_in.shape[0], w_in.shape[0]) + (rows,) * 4
     )
     return (
         layer_out,

time: 345 us -> 328 us (0.951)
  local copies, waits for them, and re-layouts: 23.7 us -> 5.21 us
  Pallas kernels: 300 us -> 318 us
  other arithmetic: 17.5 us -> 1.72 us
    reduce_sum x7 -> x0, other arithmetic: 9.13 us -> none  [the longest x3 5.55 us: layer_norm(): center = values - jnp.mean(values, axis=-1, keepdims=True)]
    slice x2 -> x0, local copies, waits for them, and re-layouts: 8.34 us -> none  [local(): sums[lo:hi]]
    pallas_call x0 -> x1, Pallas kernels: none -> 7.69 us  [widen(): pl.pallas_call(functools.partial(_widen_kernel, plan), out_shape=[jax.Sha...]
    pallas_call x1, Pallas kernels: 98.9 us -> 106 us  [gather_and_forward(): pl.pallas_call(functools.partial(_forward_kernel, sizes), out_shape=[jax....]
    another operation x8 -> x0, local copies, waits for them, and re-layouts: 4.86 us -> none  [local(): jnp.stack([b_time, b_query, b_value, b_out, gain_one, shift_one, b_down,...]
    convert_element_type x7 -> x0, other arithmetic: 4.09 us -> none  [the longest x2 0.73 us: local(): row_keep = own_valid.reshape(token_count, 1).astype(f32)]
    pallas_call x1, Pallas kernels: 201 us -> 204 us  [backward_and_reduce(): pl.pallas_call(functools.partial(_backward_kernel, dp_n, slab, 1), out_sh...]
where the time goes in v2:
time: 328 us; the launch traced here: 327 us
  Pallas kernels  318 us (97%)
  local copies, waits for them, and re-layouts  5.21 us (2%)
    pallas_call x1, Pallas kernels, backward_and_reduce(): pl.pallas_call(functools.partial(_backward_kernel, dp_n, slab, 1), out_sh...  204 us
    pallas_call x1, Pallas kernels, gather_and_forward(): pl.pallas_call(functools.partial(_forward_kernel, sizes), out_shape=[jax....  106 us
    pallas_call x1, Pallas kernels, widen(): pl.pallas_call(functools.partial(_widen_kernel, plan), out_shape=[jax.Sha...  7.69 us

profile of v2, /device:TPU:0, one launch (start us, length us, event | category | flops | bytes accessed | tf_op | source)
XLA Modules:
  0.0 327.0 jit_solution(4096755099174141498)
XLA Ops:
  0.7 105.9 %gather_and_forward.1 = (bf16[1024,1024]{1,0:T(8,128)(2,1)}, bf16[1024,1024]{1,0:T(8,128)(2,1)}, bf16[1024,1024]{1,0:T(8,128)(2,1)}, bf16[1024,1024]{1,0:T(8,128...) custom-call(bf16[256,1024]{1,0:T(8,128)(2,1)} %refs_0_.1, ...), custom_call_target="tpu_custom_call" | custom-call | tf_op jit(solution)/shard_map/gather_and_forward/pallas_call | solution.py:334
  106.6 204.4 %backward_and_reduce.1 = (bf16[3072,1024]{1,0:T(8,128)(2,1)}, f32[16,1024]{1,0:T(8,128)}, f32[2,8,2,2,8,128]{5,4,3,2,1,0:T(8,128)}, bf16[512,1024]{1,0:T(8,128)(2,1)}) custom-call(bf16[512,4096]{1,0:T(8,128)(2,1)} %get-tuple-element.50.refs_0_, bf16[512,4096]{1,0:T(8,128)(2,1)} %get-tuple-element.51.refs_1_, bf16[4096,1024]{1,0:T(8,128)(2,1)} %get-tuple-element.52.refs_2_, ...), custom_call_target="tpu_custom_call" | custom-call | tf_op jit(solution)/shard_map/backward_and_reduce/pallas_call | solution.py:905
  311.1 7.7 %widen.1 = (f32[1024,1024]{1,0:T(8,128)}, f32[1024,1024]{1,0:T(8,128)}, f32[256,1024]{1,0:T(8,128)}, f32[256,1024]{1,0:T(8,128)}, f32[256,1024]{1,0:T(8,128)}, /*index=5*/f32[256,1024]{1,0:T(8,128)}) custom-call(bf16[3072,1024]{1,0:T(8,128)(2,1)} %get-tuple-element.70.sums), custom_call_target="tpu_custom_call" | custom-call | tf_op jit(solution)/shard_map/widen/pallas_call | solution.py:983
  318.8 0.0 copy-start
  318.8 0.0 copy-start.1
  318.8 1.1 convert_element_type.7
  320.0 1.3 fusion
  321.3 1.8 fusion.7
  323.1 0.6 convert_reduce_fusion
  323.7 0.8 slice_bitcast_fusion
  324.5 0.6 copy.48
  325.1 0.0 copy-done
  325.1 1.0 copy.51
  326.1 0.0 copy-done.1
  326.1 1.0 copy.52
  (2 shorter events, 0.0 us)
Async XLA Ops:
  318.8 6.3 %copy-start = (bf16[512,1024]{1,0:T(8,128)(2,1)S(1)}, bf16[512,1024]{1,0:T(8,128)(2,1)}, u32[]{:S(2)}) copy-start(bf16[512,1024]{1,0:T(8,128)(2,1)} %get-tuple-element.108) | copy-start | bytes 3145732
  318.8 7.3 %copy-start.1 = (bf16[512,1024]{1,0:T(8,128)(2,1)S(1)}, bf16[512,1024]{1,0:T(8,128)(2,1)}, u32[]{:S(2)}) copy-start(bf16[512,1024]{1,0:T(8,128)(2,1)} %get-tuple-element.109) | copy-start | bytes 3145732

commit v3 on v2

--- a/solution.py
+++ b/solution.py
@@ -485,13 +485,30 @@
         give = pl.ds(pl.multiple_of((1 - x) * hs, 16), hs)
         return remote(own.at[k, y, give], x_in.at[k], x_s.at[k], x_r.at[k], side)
 
-    def z_copy(k, o):
-        piece = pl.ds(pl.multiple_of(x * hs + lax.rem(z + o, nz) * ps, 16), ps)
-        return remote(own.at[k, y, piece], z_in.at[k, o], z_s.at[k, o], z_r.at[k, o], others[o - 1])
-
-    def zg_copy(k, o):
-        mine = own.at[k, 1 - y, pl.ds(pl.multiple_of(x * hs + z * ps, 16), ps)]
-        return remote(mine, mine, zg_s.at[k, o], zg_r.at[k, o], others[o - 1])
+    hops = [1 << i for i in range(nz.bit_length() - 1)]
+
+    def z_rows(i, bit):
+        start = x * hs
+        for j, d in enumerate(hops[: i + 1]):
+            half = hs >> (j + 1)
+            start += (bit if j == i else lax.rem(lax.div(z, d), 2)) * half
+        return pl.ds(pl.multiple_of(start, 16), hs >> (i + 1))
+
+    def z_bit(i):
+        return lax.rem(lax.div(z, hops[i]), 2)
+
+    def z_peer(i):
+        return ((z ^ hops[i]) * 2 + x, me)
+
+    def z_land(k, i):
+        return z_in.at[k, pl.ds(hs - (hs >> i), hs >> (i + 1))]
+
+    def z_copy(k, i):
+        return remote(own.at[k, y, z_rows(i, 1 - z_bit(i))], z_land(k, i), z_s.at[k, i], z_r.at[k, i], z_peer(i))
+
+    def zg_copy(k, i):
+        mine = own.at[k, 1 - y, z_rows(i, z_bit(i))]
+        return remote(mine, mine, zg_s.at[k, i], zg_r.at[k, i], z_peer(i))
 
     def xg_copy(k):
         mine = own.at[k, 1 - y, pl.ds(pl.multiple_of(x * hs, 16), hs)]
@@ -532,28 +549,32 @@
             own[k, y, at] = (own[k, y, at].astype(f32) + x_in[k, r].astype(f32)).astype(bf16)
 
         _row_loop(hs, rs, add)
-        for o in range(1, nz):
-            z_copy(k, o).start()
-
-    def stage_z(k):
-        for o in range(1, nz):
-            z_copy(k, o).wait_recv()
+        z_copy(k, 0).start()
+
+    last = len(hops) - 1
+
+    def stage_z(i, k):
+        z_copy(k, i).wait_recv()
+        rows = z_rows(i, z_bit(i))
+        land = hs - (hs >> i)
 
         def add(r):
-            at = pl.ds(pl.multiple_of(x * hs + z * ps + r.start, 16), r.size)
-            total = own[k, y, at].astype(f32)
-            for o in range(1, nz):
-                total += z_in[k, o, r].astype(f32)
-            own[k, 1 - y, at] = total.astype(bf16)
-
-        _row_loop(ps, rs, add)
-        for o in range(1, nz):
-            zg_copy(k, o).start()
-
-    def stage_zg(k):
-        for o in range(1, nz):
-            zg_copy(k, o).wait_recv()
-        xg_copy(k).start()
+            at = pl.ds(pl.multiple_of(rows.start + r.start, 16), r.size)
+            value = own[k, y, at].astype(f32) + z_in[k, pl.ds(pl.multiple_of(land + r.start, 16), r.size)].astype(f32)
+            own[k, (1 - y) if i == last else y, at] = value.astype(bf16)
+
+        _row_loop(rows.size, min(rows.size, 32), add)
+        if i == last:
+            zg_copy(k, i).start()
+        else:
+            z_copy(k, i + 1).start()
+
+    def stage_zg(i, k):
+        zg_copy(k, i).wait_recv()
+        if i:
+            zg_copy(k, i - 1).start()
+        else:
+            xg_copy(k).start()
 
     def stage_xg(k):
         xg_copy(k).wait_recv()
@@ -776,13 +797,16 @@
         else:
             w_copy(q, 1 + nz).wait_recv()
 
-    stages = [stage_y, stage_x, stage_z, stage_zg, stage_xg]
+    stages = [stage_y, stage_x]
+    stages += [functools.partial(stage_z, i) for i in range(len(hops))]
+    stages += [functools.partial(stage_zg, i) for i in reversed(range(len(hops)))]
+    stages += [stage_xg]
     feed = 4 * groups
     per = 2 * subs
     terms_at = feed + 4
     base = 4 if fine else terms_at + 3
     small = [(feed + 4 + at, functools.partial(v_stage, i)) for i, at in enumerate((0, 1, 4, 6, 8, 9))]
-    for q, first in ((0, 2), (1, terms_at + 6)):
+    for q, first in ((0, 2), (1, terms_at + 3)):
         small += [(first + at, functools.partial(w_stage, q, i)) for i, at in enumerate((0, 3, 5, 7, 8))]
     ticks = max([base + count + lag * (len(stages) - 1)] + [at + 1 for at, _ in small])
     bound = lengths[me] + BLOCK
@@ -834,7 +858,7 @@
 
         for m in range(3):
 
-            @pl.when(t == terms_at + 3 + m)
+            @pl.when(t == terms_at + m)
             def _():
                 resid_part(m)
 
@@ -874,9 +898,9 @@
 
     def finish(k, carry):
         x_copy(k).wait_send()
-        for o in range(1, nz):
-            z_copy(k, o).wait_send()
-            zg_copy(k, o).wait_send()
+        for i in range(len(hops)):
+            z_copy(k, i).wait_send()
+            zg_copy(k, i).wait_send()
         xg_copy(k).wait_send()
         out_copy(k).wait()
         return carry
@@ -919,7 +943,7 @@
             vmem((count, 2, slab, width), bf16),
             vmem((count, slab, width), bf16),
             vmem((count, slab // 2, width), bf16),
-            vmem((count, nz, slab // 2 // nz, width), bf16),
+            vmem((count, slab // 2, width), bf16),
             vmem((4, slots, width), bf16),
             vmem((3, slots, width), bf16),
             vmem((2, width, width), bf16),
@@ -937,7 +961,7 @@
         ]
         + [dma((2, 4)), dma((4,)), dma((4,)), dma((5,))]
         + [dma((count,))] * 6
-        + [dma((count, nz))] * 4
+        + [dma((count, max(1, nz.bit_length() - 1)))] * 4
         + [dma((count,))] * 3
         + [dma((3 + nz,))] * 2
         + [dma((2, 2 + nz))] * 2,

time: 328 us -> 320 us (0.976)
  Pallas kernels: 318 us -> 311 us
    pallas_call x1, Pallas kernels: 204 us -> 197 us  [backward_and_reduce(): pl.pallas_call(functools.partial(_backward_kernel, dp_n, slab, 1), out_sh...]
where the time goes in v3:
time: 320 us; the launch traced here: 319 us
  Pallas kernels  311 us (97%)
  local copies, waits for them, and re-layouts  5.21 us (2%)
    pallas_call x1, Pallas kernels, backward_and_reduce(): pl.pallas_call(functools.partial(_backward_kernel, dp_n, slab, 1), out_sh...  197 us
    pallas_call x1, Pallas kernels, gather_and_forward(): pl.pallas_call(functools.partial(_forward_kernel, sizes), out_shape=[jax....  106 us
    pallas_call x1, Pallas kernels, widen(): pl.pallas_call(functools.partial(_widen_kernel, plan), out_shape=[jax.Sha...  7.69 us

profile of v3, /device:TPU:0, one launch (start us, length us, event | category | flops | bytes accessed | tf_op | source)
XLA Modules:
  0.0 319.5 jit_solution(1203379921914768293)
XLA Ops:
  0.7 105.9 %gather_and_forward.1 = (bf16[1024,1024]{1,0:T(8,128)(2,1)}, bf16[1024,1024]{1,0:T(8,128)(2,1)}, bf16[1024,1024]{1,0:T(8,128)(2,1)}, bf16[1024,1024]{1,0:T(8,128...) custom-call(bf16[256,1024]{1,0:T(8,128)(2,1)} %refs_0_.1, ...), custom_call_target="tpu_custom_call" | custom-call | tf_op jit(solution)/shard_map/gather_and_forward/pallas_call | solution.py:334
  106.6 196.9 %backward_and_reduce.1 = (bf16[3072,1024]{1,0:T(8,128)(2,1)}, f32[16,1024]{1,0:T(8,128)}, f32[2,8,2,2,8,128]{5,4,3,2,1,0:T(8,128)}, bf16[512,1024]{1,0:T(8,128)(2,1)}) custom-call(bf16[512,4096]{1,0:T(8,128)(2,1)} %get-tuple-element.50.refs_0_, bf16[512,4096]{1,0:T(8,128)(2,1)} %get-tuple-element.51.refs_1_, bf16[4096,1024]{1,0:T(8,128)(2,1)} %get-tuple-element.52.refs_2_, ...), custom_call_target="tpu_custom_call" | custom-call | tf_op jit(solution)/shard_map/backward_and_reduce/pallas_call | solution.py:929
  303.5 7.7 %widen.1 = (f32[1024,1024]{1,0:T(8,128)}, f32[1024,1024]{1,0:T(8,128)}, f32[256,1024]{1,0:T(8,128)}, f32[256,1024]{1,0:T(8,128)}, f32[256,1024]{1,0:T(8,128)}, /*index=5*/f32[256,1024]{1,0:T(8,128)}) custom-call(bf16[3072,1024]{1,0:T(8,128)(2,1)} %get-tuple-element.70.sums), custom_call_target="tpu_custom_call" | custom-call | tf_op jit(solution)/shard_map/widen/pallas_call | solution.py:1007
  311.2 0.0 copy-start
  311.2 0.0 copy-start.1
  311.2 1.1 convert_element_type.7
  312.4 1.3 fusion
  313.7 1.8 fusion.7
  315.5 0.6 convert_reduce_fusion
  316.2 0.8 slice_bitcast_fusion
  316.9 0.6 copy.48
  317.5 0.0 copy-done
  317.5 1.0 copy.51
  318.5 0.0 copy-done.1
  318.5 1.0 copy.52
  (2 shorter events, 0.0 us)
Async XLA Ops:
  311.2 6.3 %copy-start = (bf16[512,1024]{1,0:T(8,128)(2,1)S(1)}, bf16[512,1024]{1,0:T(8,128)(2,1)}, u32[]{:S(2)}) copy-start(bf16[512,1024]{1,0:T(8,128)(2,1)} %get-tuple-element.108) | copy-start | bytes 3145732
  311.2 7.3 %copy-start.1 = (bf16[512,1024]{1,0:T(8,128)(2,1)S(1)}, bf16[512,1024]{1,0:T(8,128)(2,1)}, u32[]{:S(2)}) copy-start(bf16[512,1024]{1,0:T(8,128)(2,1)} %get-tuple-element.109) | copy-start | bytes 3145732
